TPU v7x, 512 devices: a whole 4x4x16 slice. The times are simulated.
512 devices in a mesh: brow: 32 (over x, y, core), bcol: 16 (over z).
Axes of the slice: x: 4, y: 4, z: 16, core: 2. Of those that a mesh axis runs over, the one named last changes fastest.
Arguments:
- held_flow: float32 [19, 512, 16384], P(None, 'brow', 'bcol'), may hold values from 0.5 to 1.5
- held_heat: float32 [7, 512, 16384], P(None, 'brow', 'bcol'), may hold values from 0.5 to 1.5
- coarse_flow: bfloat16 [19, 32, 16, 4096], P(None, 'brow', 'bcol'), may hold values from 0.5 to 1.5
- coarse_heat: bfloat16 [7, 32, 16, 4096], P(None, 'brow', 'bcol'), may hold values from 0.5 to 1.5
- pair_mask: int32 [32], P('brow'), may hold values from 1 to 15, as said below
- moved_count: int32 [32, 16], P('brow', 'bcol'), may hold values from 0 to 1, as said below
- refine_src: int32 [32, 16, 4], P('brow', 'bcol'), may hold values from -1 to 255, as said below
Outputs:
- new_flow: float32 [19, 512, 16384], P(None, 'brow', 'bcol')
- new_heat: float32 [7, 512, 16384], P(None, 'brow', 'bcol')
Inputs may be any that keep to these rules, and one draw needn't show every extreme that they name: `pair_mask`: every row of devices pairs columns by XOR with its own mask. `moved_count`: both devices of a pair hold the same count; some pair trades exactly 1 block in every draw. `refine_src`: each device has exactly 2 refined slots, of 2 different octants; for each block column and octant, no parent row is named by two devices of that column.
All inputs are finite; a program needn't handle non-finite values.
Results may differ from a plain program's by a relative error of at most 0.0013.
Values may be sent and summed in bfloat16 or wider, within the bound.
A program may use at most 128 MiB of HBM per device.

v0:
```python
import jax
import jax.numpy as jnp
import numpy as np
from jax import lax
from jax.sharding import PartitionSpec as P

BS = 16
KZ = 4
MMAX = 1
NZ = 64


flow_cx = [0, 1, -1, 0, 0, 0, 0, 1, -1, 1, -1, 1, -1, 1, -1, 0, 0, 0, 0]
flow_cy = [0, 0, 0, 1, -1, 0, 0, 1, -1, -1, 1, 0, 0, 0, 0, 1, -1, 1, -1]
flow_cz = [0, 0, 0, 0, 0, 1, -1, 0, 0, 0, 0, 1, -1, -1, 1, 1, -1, -1, 1]
flow_weight = [1.0 / 3.0] + [1.0 / 18.0] * 6 + [1.0 / 36.0] * 12
flow_reverse = [0, 2, 1, 4, 3, 6, 5, 8, 7, 10, 9, 12, 11, 14, 13, 16, 15, 18, 17]
heat_cx = [0, 1, -1, 0, 0, 0, 0]
heat_cy = [0, 0, 0, 1, -1, 0, 0]
heat_cz = [0, 0, 0, 0, 0, 1, -1]
heat_weight = [0.25] + [0.125] * 6
heat_reverse = [0, 2, 1, 4, 3, 6, 5]
tau_flow = 0.8
tau_heat = 0.7
tau_flow_coarse = 0.65
tau_heat_coarse = 0.6
buoyancy = 0.01
heat_ref = 7.0


def extended_2(shard, sides, width):
    for axis, dim in sides:
        count, length = (lax.axis_size(axis), shard.shape[dim])
        up = [(i, (i + 1) % count) for i in range(count)]
        down = [(j, i) for i, j in up]
        last = lax.slice_in_dim(shard, length - width, length, axis=dim)
        initial = lax.slice_in_dim(shard, 0, width, axis=dim)
        before = lax.ppermute(last, axis, up)
        after = lax.ppermute(initial, axis, down)
        shard = jnp.concatenate([before, shard, after], axis=dim)
    return shard


def moments(lattice, forced):
    flow_pop = lattice[:19]
    heat_pop = lattice[19:]
    density = jnp.sum(flow_pop, axis=0)
    heat_value = jnp.sum(heat_pop, axis=0)
    mom_x = jnp.zeros_like(density)
    mom_y = jnp.zeros_like(density)
    mom_z = jnp.zeros_like(density)
    for channel in range(19):
        if flow_cx[channel] != 0:
            mom_x = mom_x + flow_cx[channel] * flow_pop[channel]
        if flow_cy[channel] != 0:
            mom_y = mom_y + flow_cy[channel] * flow_pop[channel]
        if flow_cz[channel] != 0:
            mom_z = mom_z + flow_cz[channel] * flow_pop[channel]
    push_up = jnp.zeros_like(density)
    if forced:
        push_up = buoyancy * density * (heat_value - heat_ref)
        mom_z = mom_z + 0.5 * push_up
    vel_x = mom_x / density
    vel_y = mom_y / density
    vel_z = mom_z / density
    return (flow_pop, heat_pop, density, heat_value, push_up, vel_x, vel_y, vel_z)


def equilibria(density, heat_value, vel_x, vel_y, vel_z):
    speed_sq = vel_x * vel_x + vel_y * vel_y + vel_z * vel_z
    flow_eq = []
    flow_dot = []
    for channel in range(19):
        along_dir = flow_cx[channel] * vel_x + flow_cy[channel] * vel_y + flow_cz[channel] * vel_z
        flow_dot.append(along_dir)
        flow_eq.append(
            flow_weight[channel]
            * density
            * (1.0 + 3.0 * along_dir + 4.5 * along_dir * along_dir - 1.5 * speed_sq)
        )
    heat_eq = []
    for channel in range(7):
        along_dir = heat_cx[channel] * vel_x + heat_cy[channel] * vel_y + heat_cz[channel] * vel_z
        heat_eq.append(heat_weight[channel] * heat_value * (1.0 + 4.0 * along_dir))
    return (flow_eq, flow_dot, heat_eq)


def collide(lattice):
    flow_pop, heat_pop, density, heat_value, push_up, vel_x, vel_y, vel_z = moments(lattice, True)
    flow_eq, flow_dot, heat_eq = equilibria(density, heat_value, vel_x, vel_y, vel_z)
    new_rows = []
    for channel in range(19):
        source = (
            (1.0 - 0.5 / tau_flow)
            * flow_weight[channel]
            * (3.0 * (flow_cz[channel] - vel_z) + 9.0 * flow_dot[channel] * flow_cz[channel])
            * push_up
        )
        new_rows.append(
            flow_pop[channel] - (flow_pop[channel] - flow_eq[channel]) / tau_flow + source
        )
    for channel in range(7):
        new_rows.append(heat_pop[channel] - (heat_pop[channel] - heat_eq[channel]) / tau_heat)
    return jnp.stack(new_rows, 0)


def explode(lattice):
    flow_pop, heat_pop, density, heat_value, push_up, vel_x, vel_y, vel_z = moments(lattice, False)
    flow_eq, flow_dot, heat_eq = equilibria(density, heat_value, vel_x, vel_y, vel_z)
    new_rows = []
    for channel in range(19):
        new_rows.append(
            flow_eq[channel]
            + tau_flow / (2.0 * tau_flow_coarse) * (flow_pop[channel] - flow_eq[channel])
        )
    for channel in range(7):
        new_rows.append(
            heat_eq[channel]
            + tau_heat / (2.0 * tau_heat_coarse) * (heat_pop[channel] - heat_eq[channel])
        )
    return jnp.stack(new_rows, 0)


def propagate(relaxed, depth):
    width_x = relaxed.shape[1] - 2
    width_y = relaxed.shape[2] // depth - 2
    span = width_y * depth
    z_place = jnp.arange(span, dtype=jnp.int32) % depth
    new_rows = []
    for channel in range(26):
        if channel < 19:
            step_x, step_y, step_z = (flow_cx[channel], flow_cy[channel], flow_cz[channel])
            reverse = flow_reverse[channel]
        else:
            step_x, step_y, step_z = (
                heat_cx[channel - 19],
                heat_cy[channel - 19],
                heat_cz[channel - 19],
            )
            reverse = 19 + heat_reverse[channel - 19]
        start_y = (1 - step_y) * depth
        moved_in = relaxed[channel, 1 - step_x : 1 - step_x + width_x, start_y : start_y + span]
        if step_z == 1:
            bounce = relaxed[reverse, 1 : 1 + width_x, depth : depth + span]
            moved_in = jnp.where(z_place == 0, bounce, jnp.roll(moved_in, 1, axis=1))
        elif step_z == -1:
            bounce = relaxed[reverse, 1 : 1 + width_x, depth : depth + span]
            moved_in = jnp.where(z_place == depth - 1, bounce, jnp.roll(moved_in, -1, axis=1))
        new_rows.append(moved_in)
    return jnp.stack(new_rows, 0)


def per_device(held_flow, held_heat, coarse_flow, coarse_heat, pair_mask, moved_count, refine_src):
    local_z = NZ
    local_x = held_flow.shape[1]
    local_y = held_flow.shape[2] // local_z
    span = local_y * local_z
    half_edge = BS // 2
    octant_cells = half_edge**3
    parent_cells = BS**3
    gathered = (
        lax.all_gather(coarse_flow, "brow", axis=1, tiled=True),
        lax.all_gather(coarse_heat, "brow", axis=1, tiled=True),
    )
    source = refine_src[0, 0]
    usable = jnp.maximum(source, 0)
    parent_row = usable // 8
    octant = usable % 8
    chosen_flow = jnp.take(gathered[0][:, :, 0], parent_row, axis=1)
    chosen_heat = jnp.take(gathered[1][:, :, 0], parent_row, axis=1)
    chosen = jnp.concatenate([chosen_flow, chosen_heat], axis=0).reshape(26, KZ * parent_cells)
    cell_ids = jnp.arange(octant_cells, dtype=jnp.int32)
    inner_a = cell_ids // (half_edge * half_edge)
    inner_b = cell_ids // half_edge % half_edge
    inner_c = cell_ids % half_edge
    slot_ids = jnp.arange(KZ, dtype=jnp.int32)[:, None]
    octant_col = octant[:, None]
    part_x = octant_col // 4 * half_edge + inner_a[None, :]
    part_y = octant_col // 2 % 2 * half_edge + inner_b[None, :]
    part_z = octant_col % 2 * half_edge + inner_c[None, :]
    source_cell = slot_ids * parent_cells + part_x * (BS * BS) + part_y * BS + part_z
    picked = jnp.take(chosen, source_cell.reshape(-1), axis=1).astype(jnp.float32)
    exploded = explode(picked)
    dest_x = np.arange(BS)[:, None]
    dest_flat = np.arange(BS * NZ)[None, :]
    dest_y = dest_flat // NZ
    dest_z = dest_flat % NZ
    upsample = (
        dest_z // BS * half_edge**3
        + dest_x // 2 * (half_edge * half_edge)
        + dest_y // 2 * half_edge
        + dest_z % BS // 2
    )
    children = jnp.take(exploded, jnp.asarray(upsample, dtype=jnp.int32), axis=1)
    held_all = jnp.concatenate([held_flow, held_heat], axis=0)
    sent_width = MMAX * BS
    outgoing = held_all.reshape(26, local_x, local_y, local_z)[:, :, :, :sent_width].reshape(
        26, local_x, local_y * sent_width
    )
    mask_value = pair_mask[0]
    partner = jnp.bitwise_xor(lax.axis_index("bcol"), mask_value)
    columns = lax.axis_size("bcol")
    target_row = jnp.arange(columns, dtype=jnp.int32) == partner
    parcel = jnp.where(target_row[:, None, None, None], outgoing[None], 0.0)
    arrived = lax.all_to_all(
        parcel.astype(jnp.bfloat16), "bcol", split_axis=0, concat_axis=0, tiled=True
    ).astype(parcel.dtype)
    incoming = lax.dynamic_index_in_dim(arrived, partner, 0, keepdims=False)
    arrival = jnp.pad(
        incoming.reshape(26, local_x, local_y, sent_width),
        ((0, 0), (0, 0), (0, 0), (0, local_z - sent_width)),
    ).reshape(26, local_x, span)
    block_of = jnp.arange(span, dtype=jnp.int32) % local_z // BS
    migrate_here = block_of < moved_count[0, 0]
    lattice = jnp.where(migrate_here, arrival, held_all)
    refined = jnp.take(source, block_of) >= 0
    lattice = jnp.where(refined, children, lattice)
    for substep in range(2):
        relaxed = collide(lattice).reshape(26, local_x, local_y, local_z)
        extended = extended_2(relaxed, (("brow", 1), ("bcol", 2)), 1)
        lattice = propagate(extended.reshape(26, local_x + 2, (local_y + 2) * local_z), local_z)
    return (lattice[:19], lattice[19:])


def solution(mesh):
    return jax.shard_map(
        per_device,
        mesh=mesh,
        in_specs=(
            P(None, "brow", "bcol"),
            P(None, "brow", "bcol"),
            P(None, "brow", "bcol", None),
            P(None, "brow", "bcol", None),
            P("brow"),
            P("brow", "bcol"),
            P("brow", "bcol", None),
        ),
        out_specs=(P(None, "brow", "bcol"), P(None, "brow", "bcol")),
        check_vma=False,
    )
```

profile of v0, /device:TPU:32, one launch (start us, length us, event | category | flops | bytes accessed | tf_op | source)
XLA Modules:
  0.0 425.5 jit_solution(2942101356989574229)
XLA Ops:
  12.9 2.3 broadcast_in_dim.175
  15.1 3.4 select_convert_fusion
  18.6 15.3 %all-to-all-start = ((bf16[16,26,16,256]{3,2,1,0:T(8,128)(2,1)}), bf16[16,26,16,256]{3,2,1,0:T(8,128)(2,1)}, u32[]{:S(2)}, u32[]{:S(2)}) async-start(bf16[16,26,16,256]{3,2,1,0:T(8,128)(2,1)} %select_convert_fusion), calls=%async_computation | async-start | bytes 6815744 | tf_op jit(solution)/shard_map/all_to_all | solution.py:205
  35.5 2.6 compare_select_fusion.3
  38.2 35.8 %all-gather.5.cloned.1.call-done = bf16[7,32,1,4096]{3,0,2,1:T(8,128)(2,1)} async-done(((bf16[7,1,1,4096]{3,0,2,1:T(8,128)(2,1)}), bf16[7,32,1,4096]{3,0,2,1:T(8,128)(2,1)}) %all-gather.5.cloned.1.call-update) | async-done | bytes 1835024 | tf_op jit(solution)/shard_map/all_gather | solution.py:163
  74.1 2.2 gather_fusion.1
  76.3 64.6 %all-gather.3.cloned.1.call-done = bf16[19,32,1,4096]{3,0,2,1:T(8,128)(2,1)} async-done(((bf16[19,1,1,4096]{3,0,2,1:T(8,128)(2,1)}), bf16[19,32,1,4096]{3,0,2,1:T(8,128)(2,1)}) %all-gather.3.cloned.1.call-update) | async-done | bytes 4980752 | tf_op jit(solution)/shard_map/all_gather | solution.py:162
  140.9 3.4 gather_fusion
  145.9 3.3 copy.764
  149.2 8.3 %gather_fusion.2 = bf16[2048,26]{1,0:T(8,128)(2,1)S(1)} fusion(bf16[26,16384]{0,1:T(8,128)(2,1)} %copy.764, s32[2048]{0:T(1024)S(1)} %broadcast_clamp_fusion.1), kind=kCustom, calls=%fused_computation.2 | custom fusion | bytes 221184 | tf_op jit(solution)/shard_map/jit(_take)/gather | solution.py:182
  159.6 54.8 %gather_fusion.3 = f32[16384,26]{1,0:T(8,128)} fusion(f32[26,2048]{0,1:T(8,128)S(1)} %copy.766, s32[16384]{0:T(1024)S(1)} %broadcast_clamp_fusion), kind=kCustom, calls=%fused_computation.3 | custom fusion | bytes 3473408 | tf_op jit(solution)/shard_map/jit(_take)/gather | solution.py:194
  214.4 6.4 %copy.912 = f32[16,1024,26]{1,0,2:T(8,128)} copy(f32[16,1024,26]{2,1,0:T(8,128)} %bitcast.451) | data formatting | bytes 3407872 | tf_op jit(solution)/shard_map/jit(_take)/gather | solution.py:194
  221.8 2.8 reshape.4132
  224.6 2.3 pad.4
  226.9 1.9 reshape.4133
  228.8 3.0 bitcast_select_fusion
  238.2 1.6 stack.226
  239.8 1.6 stack.227
  244.5 1.6 stack.230
  247.6 1.6 stack.232
  250.8 1.6 stack.234
  252.4 1.6 stack.235
  253.9 1.6 stack.236
  260.2 1.6 stack.240
  263.4 1.6 stack.242
  265.0 1.6 stack.243
  266.5 1.6 stack.244
  268.1 1.6 stack.245
  272.8 1.6 stack.248
  287.7 2.1 collective-permute-start
  289.8 6.7 %collective-permute-start.1 = (f32[26,1,16,64]{3,2,0,1:T(8,128)S(1)}, f32[26,1,16,64]{3,2,0,1:T(8,128)S(1)}, u32[]{:S(2)}, u32[]{:S(2)}) collective-permute-start(f32[26,1,16,64]{3,2,0,1:T(8,128)S(1)} %get-tuple-element.79), channel_id=1, source_target_pairs={{16,0},{32,16},{48,32},{64,48},{80,64},{96,80},{112,96},{128,112},... | collective-permute-start | bytes 319496 | tf_op jit(solution)/shard_map/ppermute | solution.py:39
  296.6 1.6 collective-permute-done
  298.1 1.8 collective-permute-done.1
  300.3 3.5 collective-permute-start.2
  303.8 2.6 collective-permute-start.3
  306.4 1.9 collective-permute-done.2
  308.3 3.5 collective-permute-done.3
  311.8 3.2 pad_maximum_fusion
  315.0 3.8 reshape.4134
  318.8 2.4 fusion.378
  322.1 1.6 fusion.379
  330.1 1.6 stack.253
  334.9 1.6 stack.256
  338.0 1.6 stack.258
  341.2 1.6 stack.260
  342.7 1.6 stack.261
  344.3 1.6 stack.262
  350.6 1.6 stack.266
  353.8 1.6 stack.268
  355.3 1.6 stack.269
  356.9 1.6 stack.270
  358.5 1.6 stack.271
  362.5 1.6 stack.275
  378.1 1.9 collective-permute-start.4
  380.1 7.0 %collective-permute-start.5 = (f32[26,1,16,64]{3,2,0,1:T(8,128)S(1)}, f32[26,1,16,64]{3,2,0,1:T(8,128)S(1)}, u32[]{:S(2)}, u32[]{:S(2)}) collective-permute-start(f32[26,1,16,64]{3,2,0,1:T(8,128)S(1)} %get-tuple-element.77), channel_id=1, source_target_pairs={{16,0},{32,16},{48,32},{64,48},{80,64},{96,80},{112,96},{128,112},... | collective-permute-start | bytes 319496 | tf_op jit(solution)/shard_map/ppermute | solution.py:39
  387.0 1.6 collective-permute-done.4
  388.6 1.8 collective-permute-done.5
  390.8 4.2 collective-permute-start.6
  395.0 2.2 collective-permute-start.7
  397.2 1.6 collective-permute-done.6
  398.8 5.4 %collective-permute-done.7 = f32[26,18,1,64]{3,2,0,1:T(1,128)S(1)} collective-permute-done((f32[26,18,1,64]{3,2,0,1:T(1,128)S(1)}, f32[26,18,1,64]{3,2,0,1:T(1,128)S(1)}, u32[]{:S(2)}, u32[]{:S(2)}) %collective-permute-start.7) | collective-permute-done | bytes 119840 | tf_op jit(solution)/shard_map/ppermute | solution.py:39
  404.3 3.2 pad_maximum_fusion.1
  407.4 3.8 reshape.4135
  413.2 2.4 fusion.376
  (297 shorter events, 86.9 us)
Async XLA Ops:
  7.2 66.9 %all-gather.5.cloned.1.call-start = ((), (), s32[]{:S(2)}) async-start(), calls=%async_computation.2 | async-start | bytes 2162688 | tf_op jit(solution)/shard_map/all_gather | solution.py:163
  7.9 133.0 %all-gather.3.cloned.1.call-start = ((), (), s32[]{:S(2)}) async-start(), calls=%async_computation.1 | async-start | bytes 6488064 | tf_op jit(solution)/shard_map/all_gather | solution.py:162
  11.7 6.8 %copy-start = (f32[26,16,1024]{2,1,0:T(8,128)}, f32[26,16,1024]{2,1,0:T(8,128)S(1)}, u32[]{:S(2)}) copy-start(f32[26,16,1024]{2,1,0:T(8,128)S(1)} %constant_dynamic-update-slice_fusion) | copy-start | bytes 5111812
  18.5 15.4 %copy-start.28 = (s32[1,1,4]{2,1,0:T(1,128)S(1)}, s32[1,1,4]{2,1,0:T(1,128)}, u32[]{:S(2)}) copy-start(s32[1,1,4]{2,1,0:T(1,128)} %param.14) | copy-start | bytes 52
  18.5 19.7 %copy-start.26 = (s32[16384]{0:T(1024)S(1)}, s32[16384]{0:T(1024)}, u32[]{:S(2)}) copy-start(s32[16384]{0:T(1024)} %constant.396) | copy-start | bytes 196612
  18.6 202.3 %all-to-all-start = ((bf16[16,26,16,256]{3,2,1,0:T(8,128)(2,1)}), bf16[16,26,16,256]{3,2,1,0:T(8,128)(2,1)}, u32[]{:S(2)}, u32[]{:S(2)}) async-start(bf16[16,26,16,256]{3,2,1,0:T(8,128)(2,1)} %select_convert_fusion), calls=%async_computation | async-start | bytes 6815744 | tf_op jit(solution)/shard_map/all_to_all | solution.py:205
  276.0 11.3 %copy-start.22 = (f32[1,16,16,64]{3,2,1,0:T(8,128)S(1)}, f32[1,16,16,64]{3,2,1,0:T(8,128)}, u32[]{:S(2)}) copy-start(f32[1,16,16,64]{3,2,1,0:T(8,128)} %stack.238) | copy-start | bytes 196612
  276.0 11.3 %copy-start.20 = (f32[1,16,16,64]{3,2,1,0:T(8,128)S(1)}, f32[1,16,16,64]{3,2,1,0:T(8,128)}, u32[]{:S(2)}) copy-start(f32[1,16,16,64]{3,2,1,0:T(8,128)} %stack.239) | copy-start | bytes 196612
  276.0 11.3 %copy-start.14 = (f32[1,16,16,64]{3,2,1,0:T(8,128)S(1)}, f32[1,16,16,64]{3,2,1,0:T(8,128)}, u32[]{:S(2)}) copy-start(f32[1,16,16,64]{3,2,1,0:T(8,128)} %stack.240) | copy-start | bytes 196612
  276.0 11.4 %copy-start.15 = (f32[1,16,16,64]{3,2,1,0:T(8,128)S(1)}, f32[1,16,16,64]{3,2,1,0:T(8,128)}, u32[]{:S(2)}) copy-start(f32[1,16,16,64]{3,2,1,0:T(8,128)} %stack.241) | copy-start | bytes 196612
  276.0 11.4 %copy-start.16 = (f32[1,16,16,64]{3,2,1,0:T(8,128)S(1)}, f32[1,16,16,64]{3,2,1,0:T(8,128)}, u32[]{:S(2)}) copy-start(f32[1,16,16,64]{3,2,1,0:T(8,128)} %stack.242) | copy-start | bytes 196612
  276.0 11.4 %copy-start.12 = (f32[1,16,16,64]{3,2,1,0:T(8,128)S(1)}, f32[1,16,16,64]{3,2,1,0:T(8,128)}, u32[]{:S(2)}) copy-start(f32[1,16,16,64]{3,2,1,0:T(8,128)} %stack.243) | copy-start | bytes 196612
  276.0 11.4 %copy-start.10 = (f32[1,16,16,64]{3,2,1,0:T(8,128)S(1)}, f32[1,16,16,64]{3,2,1,0:T(8,128)}, u32[]{:S(2)}) copy-start(f32[1,16,16,64]{3,2,1,0:T(8,128)} %stack.244) | copy-start | bytes 196612
  276.0 11.5 %copy-start.7 = (f32[1,16,16,64]{3,2,1,0:T(8,128)S(1)}, f32[1,16,16,64]{3,2,1,0:T(8,128)}, u32[]{:S(2)}) copy-start(f32[1,16,16,64]{3,2,1,0:T(8,128)} %stack.245) | copy-start | bytes 196612
  276.0 11.5 %copy-start.1 = (f32[1,16,16,64]{3,2,1,0:T(8,128)S(1)}, f32[1,16,16,64]{3,2,1,0:T(8,128)}, u32[]{:S(2)}) copy-start(f32[1,16,16,64]{3,2,1,0:T(8,128)} %stack.246) | copy-start | bytes 196612
  276.0 11.5 %copy-start.2 = (f32[1,16,16,64]{3,2,1,0:T(8,128)S(1)}, f32[1,16,16,64]{3,2,1,0:T(8,128)}, u32[]{:S(2)}) copy-start(f32[1,16,16,64]{3,2,1,0:T(8,128)} %stack.247) | copy-start | bytes 196612
  276.1 11.5 %copy-start.3 = (f32[1,16,16,64]{3,2,1,0:T(8,128)S(1)}, f32[1,16,16,64]{3,2,1,0:T(8,128)}, u32[]{:S(2)}) copy-start(f32[1,16,16,64]{3,2,1,0:T(8,128)} %stack.248) | copy-start | bytes 196612
  276.1 11.5 %copy-start.4 = (f32[1,16,16,64]{3,2,1,0:T(8,128)S(1)}, f32[1,16,16,64]{3,2,1,0:T(8,128)}, u32[]{:S(2)}) copy-start(f32[1,16,16,64]{3,2,1,0:T(8,128)} %stack.249) | copy-start | bytes 196612
  287.7 10.5 %collective-permute-start = (f32[26,1,16,64]{3,2,0,1:T(8,128)S(1)}, f32[26,1,16,64]{3,2,0,1:T(8,128)S(1)}, u32[]{:S(2)}, u32[]{:S(2)}) collective-permute-start(f32[26,1,16,64]{3,2,0,1:T(8,128)S(1)} %get-tuple-element.78), channel_id=1, source_target_pairs={{0,16},{16,32},{32,48},{48,64},{64,80},{80,96},{96,112},{112,128},... | collective-permute-start | bytes 319496 | tf_op jit(solution)/shard_map/ppermute | solution.py:38
  289.8 10.1 %collective-permute-start.1 = (f32[26,1,16,64]{3,2,0,1:T(8,128)S(1)}, f32[26,1,16,64]{3,2,0,1:T(8,128)S(1)}, u32[]{:S(2)}, u32[]{:S(2)}) collective-permute-start(f32[26,1,16,64]{3,2,0,1:T(8,128)S(1)} %get-tuple-element.79), channel_id=1, source_target_pairs={{16,0},{32,16},{48,32},{64,48},{80,64},{96,80},{112,96},{128,112},... | collective-permute-start | bytes 319496 | tf_op jit(solution)/shard_map/ppermute | solution.py:39
  300.3 8.0 %collective-permute-start.2 = (f32[26,18,1,64]{3,2,0,1:T(1,128)S(1)}, f32[26,18,1,64]{3,2,0,1:T(1,128)S(1)}, u32[]{:S(2)}, u32[]{:S(2)}) collective-permute-start(f32[26,18,1,64]{3,2,0,1:T(1,128)S(1)} %get-tuple-element.74), channel_id=1, source_target_pairs={{0,1},{1,2},{2,3},{3,4},{4,5},{5,6},{6,7},{7,8},{8,9},{9,10},{10,1... | collective-permute-start | bytes 359432 | tf_op jit(solution)/shard_map/ppermute | solution.py:38
  303.8 8.0 %collective-permute-start.3 = (f32[26,18,1,64]{3,2,0,1:T(1,128)S(1)}, f32[26,18,1,64]{3,2,0,1:T(1,128)S(1)}, u32[]{:S(2)}, u32[]{:S(2)}) collective-permute-start(f32[26,18,1,64]{3,2,0,1:T(1,128)S(1)} %get-tuple-element.75), channel_id=1, source_target_pairs={{1,0},{2,1},{3,2},{4,3},{5,4},{6,5},{7,6},{8,7},{9,8},{10,9},{11,1... | collective-permute-start | bytes 359432 | tf_op jit(solution)/shard_map/ppermute | solution.py:39
  330.1 30.0 %copy-start.25 = (f32[1,16,1024]{2,1,0:T(8,128)S(1)}, f32[1,16,1024]{2,1,0:T(8,128)}, u32[]{:S(2)}) copy-start(f32[1,16,1024]{2,1,0:T(8,128)} %get-tuple-element.255) | copy-start | bytes 196612
  330.1 30.7 %copy-start.24 = (f32[1,16,1024]{2,1,0:T(8,128)S(1)}, f32[1,16,1024]{2,1,0:T(8,128)}, u32[]{:S(2)}) copy-start(f32[1,16,1024]{2,1,0:T(8,128)} %get-tuple-element.257) | copy-start | bytes 196612
  365.6 12.1 %copy-start.23 = (f32[1,16,16,64]{3,2,1,0:T(8,128)S(1)}, f32[1,16,16,64]{3,2,1,0:T(8,128)}, u32[]{:S(2)}) copy-start(f32[1,16,16,64]{3,2,1,0:T(8,128)} %stack.265) | copy-start | bytes 196612
  365.6 12.2 %copy-start.21 = (f32[1,16,16,64]{3,2,1,0:T(8,128)S(1)}, f32[1,16,16,64]{3,2,1,0:T(8,128)}, u32[]{:S(2)}) copy-start(f32[1,16,16,64]{3,2,1,0:T(8,128)} %stack.266) | copy-start | bytes 196612
  365.6 12.2 %copy-start.17 = (f32[1,16,16,64]{3,2,1,0:T(8,128)S(1)}, f32[1,16,16,64]{3,2,1,0:T(8,128)}, u32[]{:S(2)}) copy-start(f32[1,16,16,64]{3,2,1,0:T(8,128)} %stack.267) | copy-start | bytes 196612
  365.6 12.2 %copy-start.18 = (f32[1,16,16,64]{3,2,1,0:T(8,128)S(1)}, f32[1,16,16,64]{3,2,1,0:T(8,128)}, u32[]{:S(2)}) copy-start(f32[1,16,16,64]{3,2,1,0:T(8,128)} %stack.268) | copy-start | bytes 196612
  365.6 12.3 %copy-start.19 = (f32[1,16,16,64]{3,2,1,0:T(8,128)S(1)}, f32[1,16,16,64]{3,2,1,0:T(8,128)}, u32[]{:S(2)}) copy-start(f32[1,16,16,64]{3,2,1,0:T(8,128)} %stack.269) | copy-start | bytes 196612
  365.6 12.3 %copy-start.13 = (f32[1,16,16,64]{3,2,1,0:T(8,128)S(1)}, f32[1,16,16,64]{3,2,1,0:T(8,128)}, u32[]{:S(2)}) copy-start(f32[1,16,16,64]{3,2,1,0:T(8,128)} %stack.270) | copy-start | bytes 196612
  365.7 12.3 %copy-start.11 = (f32[1,16,16,64]{3,2,1,0:T(8,128)S(1)}, f32[1,16,16,64]{3,2,1,0:T(8,128)}, u32[]{:S(2)}) copy-start(f32[1,16,16,64]{3,2,1,0:T(8,128)} %stack.271) | copy-start | bytes 196612
  365.7 12.3 %copy-start.8 = (f32[1,16,16,64]{3,2,1,0:T(8,128)S(1)}, f32[1,16,16,64]{3,2,1,0:T(8,128)}, u32[]{:S(2)}) copy-start(f32[1,16,16,64]{3,2,1,0:T(8,128)} %stack.272) | copy-start | bytes 196612
  365.7 12.3 %copy-start.9 = (f32[1,16,16,64]{3,2,1,0:T(8,128)S(1)}, f32[1,16,16,64]{3,2,1,0:T(8,128)}, u32[]{:S(2)}) copy-start(f32[1,16,16,64]{3,2,1,0:T(8,128)} %stack.273) | copy-start | bytes 196612
  365.7 12.4 %copy-start.5 = (f32[1,16,16,64]{3,2,1,0:T(8,128)S(1)}, f32[1,16,16,64]{3,2,1,0:T(8,128)}, u32[]{:S(2)}) copy-start(f32[1,16,16,64]{3,2,1,0:T(8,128)} %stack.275) | copy-start | bytes 196612
  365.7 12.4 %copy-start.6 = (f32[1,16,16,64]{3,2,1,0:T(8,128)S(1)}, f32[1,16,16,64]{3,2,1,0:T(8,128)}, u32[]{:S(2)}) copy-start(f32[1,16,16,64]{3,2,1,0:T(8,128)} %stack.276) | copy-start | bytes 196612
  378.1 10.5 %collective-permute-start.4 = (f32[26,1,16,64]{3,2,0,1:T(8,128)S(1)}, f32[26,1,16,64]{3,2,0,1:T(8,128)S(1)}, u32[]{:S(2)}, u32[]{:S(2)}) collective-permute-start(f32[26,1,16,64]{3,2,0,1:T(8,128)S(1)} %get-tuple-element.76), channel_id=1, source_target_pairs={{0,16},{16,32},{32,48},{48,64},{64,80},{80,96},{96,112},{112,128},... | collective-permute-start | bytes 319496 | tf_op jit(solution)/shard_map/ppermute | solution.py:38
  380.1 10.3 %collective-permute-start.5 = (f32[26,1,16,64]{3,2,0,1:T(8,128)S(1)}, f32[26,1,16,64]{3,2,0,1:T(8,128)S(1)}, u32[]{:S(2)}, u32[]{:S(2)}) collective-permute-start(f32[26,1,16,64]{3,2,0,1:T(8,128)S(1)} %get-tuple-element.77), channel_id=1, source_target_pairs={{16,0},{32,16},{48,32},{64,48},{80,64},{96,80},{112,96},{128,112},... | collective-permute-start | bytes 319496 | tf_op jit(solution)/shard_map/ppermute | solution.py:39
  390.8 8.0 %collective-permute-start.6 = (f32[26,18,1,64]{3,2,0,1:T(1,128)S(1)}, f32[26,18,1,64]{3,2,0,1:T(1,128)S(1)}, u32[]{:S(2)}, u32[]{:S(2)}) collective-permute-start(f32[26,18,1,64]{3,2,0,1:T(1,128)S(1)} %get-tuple-element.72), channel_id=1, source_target_pairs={{0,1},{1,2},{2,3},{3,4},{4,5},{5,6},{6,7},{7,8},{8,9},{9,10},{10,1... | collective-permute-start | bytes 359432 | tf_op jit(solution)/shard_map/ppermute | solution.py:38
  395.0 9.2 %collective-permute-start.7 = (f32[26,18,1,64]{3,2,0,1:T(1,128)S(1)}, f32[26,18,1,64]{3,2,0,1:T(1,128)S(1)}, u32[]{:S(2)}, u32[]{:S(2)}) collective-permute-start(f32[26,18,1,64]{3,2,0,1:T(1,128)S(1)} %get-tuple-element.73), channel_id=1, source_target_pairs={{1,0},{2,1},{3,2},{4,3},{5,4},{6,5},{7,6},{8,7},{9,8},{10,9},{11,1... | collective-permute-start | bytes 359432 | tf_op jit(solution)/shard_map/ppermute | solution.py:39
  417.1 0.8 copy-start.27
  417.6 1.0 copy-start.29
Sparse Core Ops, SparseCore 0:
  11.1 62.9 all-gather.4
  77.2 63.6 all-gather.2
where the time goes:
time: 429 us; the launch traced here: 426 us
  local copies, waits for them, and re-layouts  213 us (50%)
  waiting for transfers between devices  121 us (28%)
  starting transfers between devices  45.6 us (11%)
  other arithmetic  29.3 us (7%)
  between operations  16.9 us (4%)
    another operation x54, local copies, waits for them, and re-layouts, collide(): return jnp.stack(new_rows, 0)  75 us
    all_gather x1, waiting for transfers between devices, per_device(): lax.all_gather(coarse_flow, 'brow', axis=1, tiled=True)  64.6 us
    gather x2, local copies, waits for them, and re-layouts, per_device(): jnp.take(exploded, jnp.asarray(upsample, dtype=jnp.int32), axis=1)  61.2 us
    all_gather x1, waiting for transfers between devices, per_device(): lax.all_gather(coarse_heat, 'brow', axis=1, tiled=True)  35.8 us
    unnamed x153, local copies, waits for them, and re-layouts  28.3 us
    ppermute x4, starting transfers between devices, extended_2(): after = lax.ppermute(initial, axis, down)  18.5 us
    all_to_all x1, starting transfers between devices, per_device(): lax.all_to_all(parcel.astype(jnp.bfloat16), 'bcol', split_axis=0, concat_...  15.3 us
    ppermute x4, waiting for transfers between devices, extended_2(): after = lax.ppermute(initial, axis, down)  12.4 us
  transfers between devices with their start and end apart: 11, of which 10 were waited for; matrix products, arithmetic and copies ran while one was open for 22% of the time, Pallas kernels for 0%

commit v1 on v0

v1 whole, which is shorter than its diff:
```python
import jax
import jax.numpy as jnp
import numpy as np
from jax import lax
from jax.experimental import pallas as pl
from jax.experimental.pallas import tpu as pltpu
from jax.sharding import PartitionSpec as P

MESH = pl.DeviceIdType.MESH
F32 = jnp.float32
BF16 = jnp.bfloat16

NPOP = 26
LX = 16
LANES = 1024
RING = 16
STEPS = 8
SPLITS = ((0, 9), (9, 18), (18, 26))
ROWS_A, ROWS_B = 64, 48

flow_cx = [0, 1, -1, 0, 0, 0, 0, 1, -1, 1, -1, 1, -1, 1, -1, 0, 0, 0, 0]
flow_cy = [0, 0, 0, 1, -1, 0, 0, 1, -1, -1, 1, 0, 0, 0, 0, 1, -1, 1, -1]
flow_cz = [0, 0, 0, 0, 0, 1, -1, 0, 0, 0, 0, 1, -1, -1, 1, 1, -1, -1, 1]
flow_weight = [1.0 / 3.0] + [1.0 / 18.0] * 6 + [1.0 / 36.0] * 12
flow_reverse = [0, 2, 1, 4, 3, 6, 5, 8, 7, 10, 9, 12, 11, 14, 13, 16, 15, 18, 17]
heat_reverse = [0, 2, 1, 4, 3, 6, 5]
POP_CX = flow_cx + flow_cx[:7]
POP_CY = flow_cy + flow_cy[:7]
POP_CZ = flow_cz + flow_cz[:7]
POP_REV = flow_reverse + [19 + r for r in heat_reverse]
X_UP = [i for i in range(NPOP) if POP_CX[i] == 1]
X_DOWN = [i for i in range(NPOP) if POP_CX[i] == -1]
Y_UP = [i for i in range(NPOP) if POP_CY[i] == 1]
Y_DOWN = [i for i in range(NPOP) if POP_CY[i] == -1]
CORNERS = ((7, 1, 1), (8, -1, -1), (9, 1, -1), (10, -1, 1))
tau_flow = 0.8
tau_heat = 0.7
tau_flow_coarse = 0.65
tau_heat_coarse = 0.6
buoyancy = 0.01
heat_ref = 7.0


def ring_seats(mask):
    packets = []
    for c in range(RING):
        d = ((c ^ mask) - c) % RING
        if d < STEPS:
            packets += [(d, c, 0), (d, c, 1)]
        elif d == STEPS:
            packets += [(d, c, 0)]
    packets.sort(key=lambda p: (-p[0], p[1], p[2]))
    busy = {}
    out = {}

    def place(n):
        if n == len(packets):
            return True
        d, c, h = packets[n]
        first = out[(c, 0)] + 1 if h == 1 else 0
        for t0 in range(first, STEPS - d + 1):
            taken = busy.setdefault((c - t0) % RING, [])
            if all(t0 + d <= a or b <= t0 for a, b in taken):
                taken.append((t0, t0 + d))
                out[(c, h)] = t0
                if place(n + 1):
                    return True
                taken.pop()
                del out[(c, h)]
        return False

    assert place(0)
    return out


def ring_tables():
    send = np.zeros((RING, RING, 2, STEPS), np.int64)
    land = np.zeros((RING, RING, 2), np.int64)
    send[:, :, :, 0] = 1
    for mask in range(1, RING):
        up = ring_seats(mask)
        for (c, h), t0 in up.items():
            d = ((c ^ mask) - c) % RING
            send[mask, c, 0, t0] = 1 + h
            land[mask, c ^ mask, h] = t0 + d - 1
            mc = RING - 1 - c
            mh = 1 if d == STEPS else h
            send[mask, mc, 1, t0] = 1 + mh
            land[mask, mc ^ mask, mh] = STEPS + t0 + d - 1
    word = np.zeros((RING, RING), np.int64)
    for t in range(STEPS):
        word |= send[:, :, 0, t] << (2 * t)
        word |= send[:, :, 1, t] << (16 + 2 * t)
    word = np.where(word >= 2**31, word - 2**32, word).astype(np.int32)
    return np.stack([word.reshape(-1), land[:, :, 0].reshape(-1).astype(np.int32),
                     land[:, :, 1].reshape(-1).astype(np.int32)])


RING_TABLE = ring_tables()


def lane_ids(rows):
    return lax.broadcasted_iota(jnp.int32, (rows, 128), 1)


def total(values):
    values = list(values)
    while len(values) > 1:
        values = [a + b for a, b in zip(values[::2], values[1::2])] + (
            [values[-1]] if len(values) % 2 else [])
    return values[0]


def moments(f, push):
    rho = total(f[:19])
    heat = total(f[19:])

    def along(c):
        ups = [f[i] for i in range(19) if c[i] == 1]
        downs = [f[i] for i in range(19) if c[i] == -1]
        return total([u - d for u, d in zip(ups, downs)])

    mx, my, mz = along(flow_cx), along(flow_cy), along(flow_cz)
    force = None
    if push:
        force = buoyancy * rho * (heat - heat_ref)
        mz = mz + 0.5 * force
    inv = 1.0 / rho
    return rho, heat, force, (mx, my, mz), (mx * inv, my * inv, mz * inv)


def dot_dir(i, v):
    terms = []
    for c, a in zip((flow_cx[i], flow_cy[i], flow_cz[i]), v):
        if c:
            terms.append((c, a))
    out = terms[0][1] if terms[0][0] > 0 else -terms[0][1]
    for c, a in terms[1:]:
        out = out + a if c > 0 else out - a
    return out


PAIRS = [(1, 2), (3, 4), (5, 6), (7, 8), (9, 10), (11, 12), (13, 14), (15, 16), (17, 18)]


def collide(f):
    rho, heat, force, mom, vel = moments(f, True)
    rate = 1.0 / tau_flow
    keep = 1.0 - rate
    gain = 1.0 - 0.5 / tau_flow
    speed = mom[0] * vel[0] + mom[1] * vel[1] + mom[2] * vel[2]
    common = rate * rho - (1.5 * rate) * speed - (3.0 * gain) * force * vel[2]
    fgain = (9.0 * gain) * force
    fodd = (3.0 * gain) * force
    out = [None] * NPOP
    out[0] = keep * f[0] + flow_weight[0] * common
    for i, j in PAIRS:
        w = flow_weight[i]
        cu = dot_dir(i, vel)
        cm = dot_dir(i, mom)
        bracket = (4.5 * rate) * cm
        odd = (3.0 * rate) * cm
        if flow_cz[i] == 1:
            bracket = bracket + fgain
            odd = odd + fodd
        elif flow_cz[i] == -1:
            bracket = bracket - fgain
            odd = odd - fodd
        even = common + bracket * cu
        out[i] = keep * f[i] + w * (even + odd)
        out[j] = keep * f[j] + w * (even - odd)
    hrate = 1.0 / tau_heat
    hkeep = 1.0 - hrate
    out[19] = hkeep * f[19] + (0.25 * hrate) * heat
    side = (0.125 * hrate) * heat
    for k, a in zip((20, 22, 24), vel):
        tilt = 4.0 * side * a
        out[k] = hkeep * f[k] + (side + tilt)
        out[k + 1] = hkeep * f[k + 1] + (side - tilt)
    return out


def explode(f):
    rho, heat, _, mom, vel = moments(f, False)
    blend = tau_flow / (2.0 * tau_flow_coarse)
    rest = 1.0 - blend
    speed = mom[0] * vel[0] + mom[1] * vel[1] + mom[2] * vel[2]
    common = rest * rho - (1.5 * rest) * speed
    out = [None] * NPOP
    out[0] = blend * f[0] + flow_weight[0] * common
    for i, j in PAIRS:
        w = flow_weight[i]
        cu = dot_dir(i, vel)
        cm = dot_dir(i, mom)
        even = common + ((4.5 * rest) * cm) * cu
        odd = (3.0 * rest) * cm
        out[i] = blend * f[i] + w * (even + odd)
        out[j] = blend * f[j] + w * (even - odd)
    hblend = tau_heat / (2.0 * tau_heat_coarse)
    hrest = 1.0 - hblend
    out[19] = hblend * f[19] + (0.25 * hrest) * heat
    side = (0.125 * hrest) * heat
    for k, a in zip((20, 22, 24), vel):
        tilt = 4.0 * side * a
        out[k] = hblend * f[k] + (side + tilt)
        out[k + 1] = hblend * f[k + 1] + (side - tilt)
    return out


def held_tile(hf, hh, p, rows, cols):
    return hf[p, rows, cols] if p < 19 else hh[p - 19, rows, cols]


def pack_trade(hf, hh, own):
    group = lane_ids(LX) % 64 // 16
    for p in range(NPOP):
        for q in range(2):
            packed = None
            for kk in range(4):
                k = 4 * q + kk
                tile = held_tile(hf, hh, p, slice(None), slice(128 * k, 128 * k + 128))
                if kk == 0:
                    packed = tile
                else:
                    packed = jnp.where(group == kk, pltpu.roll(tile, 16 * kk, 1), packed)
            own[q, p] = packed.astype(BF16)


def pack_coarse(cf, ch, spread, put):
    for t in range(32):
        cols = slice(128 * t, 128 * t + 128)
        flow = cf[:, cols].astype(F32)
        heat = ch[:, cols].astype(F32)
        spread[pl.ds(t, 8, stride=32), :] = flow[0:8]
        spread[pl.ds(8 * 32 + t, 8, stride=32), :] = flow[8:16]
        spread[pl.ds(16 * 32 + t, 3, stride=32), :] = flow[16:19]
        spread[pl.ds(19 * 32 + t, 7, stride=32), :] = heat
    high = lane_ids(8) // 8 % 2 == 1
    zeros = jnp.zeros((8, 128), F32)
    for ox in range(2):
        for oy in range(2):
            low_rows, high_rows = [], []
            for pair in range(13):
                a = spread[pl.ds(pair * 32 + 16 * ox + oy, 8, stride=2), :]
                b = spread[pl.ds((pair + 13) * 32 + 16 * ox + oy, 8, stride=2), :]
                low_rows.append(jnp.where(high, pltpu.roll(b, 8, 1), a))
                high_rows.append(jnp.where(high, b, pltpu.roll(a, 120, 1)))
            for oz, rows in ((0, low_rows), (1, high_rows)):
                rows = rows + [zeros]
                for i in range(7):
                    put(4 * ox + 2 * oy + oz, i,
                        jnp.concatenate([rows[2 * i], rows[2 * i + 1]], axis=0).astype(BF16))


def pack_kernel(hf, hh, cf, ch, own, part_a, part_b, spread):
    pack_trade(hf, hh, own)

    def put(octant, i, value):
        if i < 4:
            part_a[octant, 16 * i:16 * i + 16, :] = value
        else:
            part_b[octant, 16 * (i - 4):16 * (i - 4) + 16, :] = value

    pack_coarse(cf, ch, spread, put)


def place():
    me = lax.axis_index("brow")
    col = lax.axis_index("bcol")
    return me // 8, me // 2 % 4, me % 2, col


def row_of(x, y, k):
    return (x * 4 + y) * 2 + k


OFFSETS = [(d, dk) for d in range(4) for dk in range(2)]


def blocks_kernel(table, mask_ref, codes_in, own, part_a, part_b,
                  arrived, picked_a, picked_b,
                  landing, leaving, held_a, held_b, codes, stage_a, stage_b, got_a, got_b,
                  ring_send, ring_recv, code_send, code_recv, one_send, one_recv,
                  two_send, two_recv):
    x, y, k, col = place()
    me = row_of(x, y, k)
    cols = ((col + 1) % RING, (col + RING - 1) % RING)
    x_group = [row_of(x, (y + d) % 4, (k + dk) % 2) for d, dk in OFFSETS]
    y_group = [row_of((x + d) % 4, y, (k + dk) % 2) for d, dk in OFFSETS]
    peers = x_group[1:] + y_group[2:]

    barrier = pltpu.get_barrier_semaphore()
    for c in cols:
        pl.semaphore_signal(barrier, inc=1, device_id=(me, c), device_id_type=MESH)
    for peer in peers:
        pl.semaphore_signal(barrier, inc=1, device_id=(peer, col), device_id_type=MESH)
    pl.semaphore_wait(barrier, 2 + len(peers))

    pending = []

    def send(source, target, sends, recvs, device):
        copy = pltpu.make_async_remote_copy(
            src_ref=source, dst_ref=target, send_sem=sends, recv_sem=recvs,
            device_id=device, device_id_type=MESH)
        copy.start()
        pending.append(copy)
        return copy

    entry = mask_ref[0] * RING + col
    word = table[0, entry]
    ring = {}

    def ring_step(step):
        for s, (lo, hi) in enumerate(SPLITS):
            for way in range(2):
                code = (word >> (16 * way + 2 * step)) & 3
                other = own[0, lo:hi]
                if step:
                    ring[way, step - 1, s].wait_recv()
                    other = jnp.where(code == 1, other, landing[way * STEPS + step - 1, lo:hi])
                slot = way * STEPS + step
                leaving[slot, lo:hi] = jnp.where(code == 2, own[1, lo:hi], other)
                ring[way, step, s] = send(
                    leaving.at[slot, lo:hi], landing.at[slot, lo:hi],
                    ring_send.at[slot, s], ring_recv.at[slot, s], (me, cols[way]))

    ring_step(0)
    code_copies = [send(codes_in, codes.at[n], code_send.at[n], code_recv.at[n], (peer, col))
                   for n, peer in enumerate(peers)]
    one_copies = []
    for d in (2, 1, 3):
        one_copies.append(send(part_a, held_a.at[d], one_send.at[0, d], one_recv.at[0, d],
                               (x_group_of(x, y, k, d), col)))
        one_copies.append(send(part_b, held_b.at[d], one_send.at[1, d], one_recv.at[1, d],
                               (row_of(x, (y + d) % 4, k), col)))
    held_a[0] = part_a[...]
    held_b[0] = part_b[...]
    ring_step(1)
    ring_step(2)
    ring_step(3)

    for copy in code_copies + one_copies:
        copy.wait_recv()

    def wanted(n):
        values = [codes_in[0, 0, j] if n is None else codes[n, 0, 0, j] for j in range(4)]
        first = values[3]
        last = values[0]
        for j in (2, 1, 0):
            first = jnp.where(values[j] >= 0, values[j], first)
        for j in (1, 2, 3):
            last = jnp.where(values[j] >= 0, values[j], last)
        return first, last

    mine = wanted(None)
    two_copies = []
    for n, (d, dk) in enumerate(OFFSETS):
        for part, (group, stage, got, held, home) in enumerate((
                (x_group, stage_a, got_a, held_a, x), (y_group, stage_b, got_b, held_b, y))):
            if n == 0:
                pair = mine
            else:
                back = OFFSETS.index(((4 - d) % 4, dk))
                pair = wanted(back - 1 if part == 0 or d == 0 else 7 + back - 2)
            for s, code in enumerate(pair):
                parent = (code >> 6) & 3 if part == 0 else (code >> 4) & 3
                value = held[(home - parent + 4) & 3, code & 7]
                if n == 0:
                    got[0, s] = value
                else:
                    stage[n, s] = value
            if n:
                two_copies.append(send(stage.at[n], got.at[n], two_send.at[part, n],
                                       two_recv.at[part, n], (group[n], col)))
    for step in range(4, STEPS):
        ring_step(step)

    for copy in two_copies:
        copy.wait_recv()
    for s, code in enumerate(mine):
        core = ((code >> 3) & 1) ^ k
        picked_a[s] = got_a[((y - ((code >> 4) & 3) + 4) & 3) * 2 + core, s]
        picked_b[s] = got_b[((x - ((code >> 6) & 3) + 4) & 3) * 2 + core, s]
    for way in range(2):
        for s in range(len(SPLITS)):
            ring[way, STEPS - 1, s].wait_recv()
    for h in range(2):
        arrived[h] = landing[table[1 + h, entry]]
    for copy in pending:
        copy.wait_send()


def x_group_of(x, y, k, d):
    return row_of((x + d) % 4, y, k)


def edge_faces(field, xs, ys, cs, base, lead):
    low = lane_ids(LX) < 64
    for n, p in enumerate(X_UP):
        xs[0, n:n + 1, :] = field[p, base + 15:base + 16, lead:lead + LANES]
    for n, p in enumerate(X_DOWN):
        xs[1, n:n + 1, :] = field[p, base:base + 1, lead:lead + LANES]
    rows = slice(base, base + LX)
    last = slice(lead + LANES - 128, lead + LANES)
    first = slice(lead, lead + 128)
    for n in range(3):
        a, b = Y_UP[2 * n], Y_UP[2 * n + 1]
        ys[0, n] = jnp.where(low, pltpu.roll(field[a, rows, last], 64, 1), field[b, rows, last])
        a, b = Y_DOWN[2 * n], Y_DOWN[2 * n + 1]
        ys[1, n] = jnp.where(low, field[a, rows, first], pltpu.roll(field[b, rows, first], 64, 1))
    for n, (p, sx, sy) in enumerate(CORNERS):
        cs[n] = field[p, base + 8:base + 16, last] if (sx, sy) == (1, 1) else (
            field[p, base:base + 8, first] if (sx, sy) == (-1, -1) else (
                field[p, base + 8:base + 16, first] if (sx, sy) == (1, -1) else
                field[p, base:base + 8, last]))


def widen(relaxed, xr, yr, cr, wide):
    for p in range(NPOP):
        wide[p, 8:24, 128:128 + LANES] = relaxed[p]
    fill_edges(xr, yr, cr, wide)


def fill_edges(xr, yr, cr, wide):
    for n, (p, sx, sy) in enumerate(CORNERS):
        rows = slice(0, 8) if sx == 1 else slice(24, 32)
        cols = slice(0, 128) if sy == 1 else slice(128 + LANES, 256 + LANES)
        wide[p, rows, cols] = cr[n]
    for n, p in enumerate(X_UP):
        wide[p, 7:8, 128:128 + LANES] = xr[0, n:n + 1, :]
    for n, p in enumerate(X_DOWN):
        wide[p, 24:25, 128:128 + LANES] = xr[1, n:n + 1, :]
    for n in range(3):
        a, b = Y_UP[2 * n], Y_UP[2 * n + 1]
        wide[a, 8:24, 0:128] = pltpu.roll(yr[0, n], 64, 1)
        wide[b, 8:24, 0:128] = yr[0, n]
        a, b = Y_DOWN[2 * n], Y_DOWN[2 * n + 1]
        wide[a, 8:24, 128 + LANES:256 + LANES] = yr[1, n]
        wide[b, 8:24, 128 + LANES:256 + LANES] = pltpu.roll(yr[1, n], 64, 1)


def pulled(wide, p, rt, k):
    cx, cy, cz = POP_CX[p], POP_CY[p], POP_CZ[p]
    rows = slice(8 + 8 * rt - cx, 16 + 8 * rt - cx)

    def tile(e):
        return pl.ds(pl.multiple_of(128 * e, 128), 128)

    low = lane_ids(8) < 64
    value = wide[p, rows, tile(k + 1)]
    shift = 0
    if cy == 1:
        value = jnp.where(low, value, wide[p, rows, tile(k)])
        shift = 64
    elif cy == -1:
        value = jnp.where(low, wide[p, rows, tile(k + 2)], value)
        shift = 64
    shift = (shift + cz) % 128
    if shift:
        value = pltpu.roll(value, shift, 1)
    if cz:
        wall = lane_ids(8) % 64 == (0 if cz == 1 else 63)
        back = wide[POP_REV[p], 8 + 8 * rt:16 + 8 * rt, tile(k + 1)]
        value = jnp.where(wall, back, value)
    return value


def start_kernel(codes_in, moved, hf, hh, arrived, picked_a, picked_b,
                 relaxed, xs, ys, cs, spread, left, right, fresh):
    high = lane_ids(8) // 8 % 2 == 1
    values = [None] * NPOP
    for pair in range(13):
        part, row = (picked_a, 8 * pair) if pair < 8 else (picked_b, 8 * pair - 64)
        base = row // 16 * 16
        a = part[0, base:base + 16, :].astype(F32)[row - base:row - base + 8]
        b = part[1, base:base + 16, :].astype(F32)[row - base:row - base + 8]
        values[pair] = jnp.where(high, pltpu.roll(b, 8, 1), a)
        values[pair + 13] = jnp.where(high, b, pltpu.roll(a, 120, 1))
    for p, value in enumerate(explode(values)):
        spread[pl.ds(16 * p, 8, stride=2), :] = value
        spread[pl.ds(16 * p + 1, 8, stride=2), :] = value
    for p in range(NPOP):
        rows = slice(16 * p, 16 * p + 16)
        value = spread[rows, :]
        top = value.astype(BF16)
        left[rows, 0:128] = top
        left[rows, 128:256] = (value - top.astype(F32)).astype(BF16)
        left[rows, 256:384] = arrived[0, p]
        left[rows, 384:512] = arrived[1, p]

    source = [codes_in[0, 0, j] for j in range(4)]
    refined = [jnp.where(v >= 0, 1, 0) for v in source]
    rank = [0]
    for j in range(3):
        rank.append(rank[-1] + refined[j])
    child = [jnp.where(refined[j] == 1, rank[j] * 8, 1 << 20) for j in range(4)]
    trade = jnp.where((moved[0, 0] > 0) & (refined[0] == 0), 0, 1 << 20)

    def by_slot(lane, picks):
        slot = lane % 64 // 16
        return jnp.where(slot == 0, picks[0], jnp.where(
            slot == 1, picks[1], jnp.where(slot == 2, picks[2], picks[3])))

    for t in range(8):
        lane = lax.broadcasted_iota(jnp.int32, (1, 128), 1)
        yy = 2 * t + lane // 64
        want = yy // 2 * 16 + lane % 16 // 2 + by_slot(lane, child)
        row = lax.broadcasted_iota(jnp.int32, (128, 128), 0)
        hot = jnp.where(row == want, 1.0, 0.0).astype(BF16)
        cols = slice(128 * t, 128 * t + 128)
        right[0:128, cols] = hot
        right[128:256, cols] = hot
        row = lax.broadcasted_iota(jnp.int32, (256, 128), 0)
        z = lane % 64
        want = yy // 8 * 128 + yy % 2 * 64 + yy % 8 // 2 * 16 + z
        want = jnp.where(z < 16, want + trade, 1 << 20)
        right[256:512, cols] = jnp.where(row == want, 1.0, 0.0).astype(BF16)
    for t in range(4):
        cols = slice(256 * t, 256 * t + 256)
        fresh[:, cols] = jnp.dot(left[...], right[:, cols], preferred_element_type=F32)

    keep = [jnp.where(refined[j] == 1, 0, 1) for j in range(4)]
    keep[0] = jnp.where(moved[0, 0] > 0, 0, keep[0])
    kept = by_slot(lane_ids(8), keep) == 1

    def body(k, carry):
        cols = pl.ds(pl.multiple_of(128 * k, 128), 128)
        for rt in range(2):
            rows = slice(8 * rt, 8 * rt + 8)
            f = [jnp.where(kept, held_tile(hf, hh, p, rows, cols),
                           fresh[16 * p + 8 * rt:16 * p + 8 * rt + 8, cols])
                 for p in range(NPOP)]
            for p, value in enumerate(collide(f)):
                relaxed[p, rows, cols] = value
        return carry

    lax.fori_loop(0, 8, body, 0)
    edge_faces(relaxed, xs, ys, cs, 0, 0)


def step_kernel(relaxed_in, xr, yr, cr, relaxed, xs, ys, cs, wide):
    widen(relaxed_in, xr, yr, cr, wide)

    def body(k, carry):
        cols = pl.ds(pl.multiple_of(128 * k, 128), 128)
        for rt in range(2):
            f = [pulled(wide, p, rt, k) for p in range(NPOP)]
            for p, value in enumerate(collide(f)):
                relaxed[p, 8 * rt:8 * rt + 8, cols] = value
        return carry

    lax.fori_loop(0, 8, body, 0)
    edge_faces(relaxed, xs, ys, cs, 0, 0)


def final_kernel(relaxed_in, xr, yr, cr, out_flow, out_heat, wide):
    widen(relaxed_in, xr, yr, cr, wide)

    def body(k, carry):
        cols = pl.ds(pl.multiple_of(128 * k, 128), 128)
        for rt in range(2):
            for p in range(NPOP):
                value = pulled(wide, p, rt, k)
                if p < 19:
                    out_flow[p, 8 * rt:8 * rt + 8, cols] = value
                else:
                    out_heat[p - 19, 8 * rt:8 * rt + 8, cols] = value
        return carry

    lax.fori_loop(0, 8, body, 0)


def halo_kernel(xs, ys, cs, xr, yr, cr, send_sem, recv_sem):
    row = lax.axis_index("brow")
    col = lax.axis_index("bcol")
    rows = {1: (row + 1) % 32, -1: (row + 31) % 32, 0: row}
    cols = {1: (col + 1) % RING, -1: (col + RING - 1) % RING, 0: col}
    moves = [(xs.at[0], xr.at[0], 1, 0), (xs.at[1], xr.at[1], -1, 0),
             (ys.at[0], yr.at[0], 0, 1), (ys.at[1], yr.at[1], 0, -1)]
    for n, (p, sx, sy) in enumerate(CORNERS):
        moves.append((cs.at[n], cr.at[n], sx, sy))
    barrier = pltpu.get_barrier_semaphore()
    for _, _, sx, sy in moves:
        pl.semaphore_signal(barrier, inc=1, device_id=(rows[sx], cols[sy]), device_id_type=MESH)
    pl.semaphore_wait(barrier, len(moves))
    copies = []
    for n, (source, target, sx, sy) in enumerate(moves):
        copy = pltpu.make_async_remote_copy(
            src_ref=source, dst_ref=target, send_sem=send_sem.at[n], recv_sem=recv_sem.at[n],
            device_id=(rows[sx], cols[sy]), device_id_type=MESH)
        copy.start()
        copies.append(copy)
    for copy in copies:
        copy.wait()


VMEM = pl.BlockSpec(memory_space=pltpu.VMEM)
SMEM = pl.BlockSpec(memory_space=pltpu.SMEM)


def struct(shape, dtype=F32):
    return jax.ShapeDtypeStruct(shape, dtype)


FACES = [struct((2, 8, LANES)), struct((2, 3, LX, 128)), struct((4, 8, 128))]
FIELD = struct((NPOP, LX, LANES))
WIDE = pltpu.VMEM((NPOP, 32, LANES + 256), F32)


def call(kernel, ins, outs, scratch, **params):
    return pl.pallas_call(
        kernel, out_shape=outs, in_specs=ins,
        out_specs=jax.tree.map(lambda _: VMEM, outs), scratch_shapes=scratch,
        compiler_params=pltpu.CompilerParams(vmem_limit_bytes=56 * 2**20, **params))


def halo(faces, number):
    sem = pltpu.SemaphoreType.DMA((8,))
    return call(halo_kernel, [VMEM] * 3, FACES, [sem, sem],
                collective_id=number, has_side_effects=True)(*faces)


def per_device(held_flow, held_heat, coarse_flow, coarse_heat, pair_mask, moved_count, refine_src):
    dma = pltpu.SemaphoreType.DMA
    own, part_a, part_b = call(
        pack_kernel, [VMEM] * 4,
        [struct((2, NPOP, LX, 128), BF16), struct((8, ROWS_A, 128), BF16),
         struct((8, ROWS_B, 128), BF16)],
        [pltpu.VMEM((NPOP * 32, 128), F32)])(
            held_flow, held_heat, coarse_flow.reshape(19, 4096), coarse_heat.reshape(7, 4096))
    ns = len(SPLITS)
    arrived, picked_a, picked_b = call(
        blocks_kernel, [SMEM] * 3 + [VMEM] * 3,
        [struct((2, NPOP, LX, 128), BF16), struct((2, ROWS_A, 128), BF16),
         struct((2, ROWS_B, 128), BF16)],
        [pltpu.VMEM((2 * STEPS, NPOP, LX, 128), BF16), pltpu.VMEM((2 * STEPS, NPOP, LX, 128), BF16),
         pltpu.VMEM((4, 8, ROWS_A, 128), BF16), pltpu.VMEM((4, 8, ROWS_B, 128), BF16),
         pltpu.SMEM((13, 1, 1, 4), jnp.int32),
         pltpu.VMEM((8, 2, ROWS_A, 128), BF16), pltpu.VMEM((8, 2, ROWS_B, 128), BF16),
         pltpu.VMEM((8, 2, ROWS_A, 128), BF16), pltpu.VMEM((8, 2, ROWS_B, 128), BF16),
         dma((2 * STEPS, ns)), dma((2 * STEPS, ns)), dma((13,)), dma((13,)),
         dma((2, 4)), dma((2, 4)), dma((2, 8)), dma((2, 8))],
        collective_id=0, has_side_effects=True)(
            jnp.asarray(RING_TABLE), pair_mask, refine_src, own, part_a, part_b)
    relaxed, *faces = call(
        start_kernel, [SMEM] * 2 + [VMEM] * 5, [FIELD] + FACES,
        [pltpu.VMEM((NPOP * LX, 128), F32), pltpu.VMEM((NPOP * LX, 512), BF16),
         pltpu.VMEM((512, LANES), BF16), pltpu.VMEM((NPOP * LX, LANES), F32)])(
            refine_src, moved_count, held_flow, held_heat, arrived, picked_a, picked_b)
    faces = halo(faces, 1)
    relaxed, *faces = call(step_kernel, [VMEM] * 4, [FIELD] + FACES, [WIDE])(relaxed, *faces)
    faces = halo(faces, 2)
    return tuple(call(final_kernel, [VMEM] * 4,
                      [struct((19, LX, LANES)), struct((7, LX, LANES))], [WIDE])(relaxed, *faces))


def solution(mesh):
    return jax.shard_map(
        per_device,
        mesh=mesh,
        in_specs=(
            P(None, "brow", "bcol"),
            P(None, "brow", "bcol"),
            P(None, "brow", "bcol", None),
            P(None, "brow", "bcol", None),
            P("brow"),
            P("brow", "bcol"),
            P("brow", "bcol", None),
        ),
        out_specs=(P(None, "brow", "bcol"), P(None, "brow", "bcol")),
        check_vma=False,
    )
```

time: 429 us -> 83.3 us (0.19)
  local copies, waits for them, and re-layouts: 213 us -> 0 us
  waiting for transfers between devices: 121 us -> 0 us
  Pallas kernels: 0 us -> 80.9 us
  starting transfers between devices: 45.6 us -> 0 us
  other arithmetic: 29.3 us -> 0 us
  between operations: 16.9 us -> 1.95 us
    all_gather x2 -> x0, waiting for transfers between devices: 100 us -> none  [the longest x1 64.6 us: per_device(): lax.all_gather(coarse_flow, 'brow', axis=1, tiled=True)]
    pallas_call x0 -> x7, Pallas kernels: none -> 80.9 us  [the longest x1 43.4 us: per_device(): call(blocks_kernel, [SMEM] * 3 + [VMEM] * 3, [struct((2, NPOP, LX, 128),...]
    gather x8 -> x0, local copies, waits for them, and re-layouts: 76.5 us -> none  [the longest x2 61.2 us: per_device(): jnp.take(exploded, jnp.asarray(upsample, dtype=jnp.int32), axis=1)]
    another operation x56 -> x0, local copies, waits for them, and re-layouts: 75.7 us -> none  [the longest x54 75 us: collide(): return jnp.stack(new_rows, 0)]
    ppermute x8 -> x0, starting transfers between devices: 30.2 us -> none  [the longest x4 18.5 us: extended_2(): after = lax.ppermute(initial, axis, down)]
    unnamed x153 -> x0, local copies, waits for them, and re-layouts: 28.3 us -> none
    ppermute x8 -> x0, waiting for transfers between devices: 19.1 us -> none  [the longest x4 12.4 us: extended_2(): after = lax.ppermute(initial, axis, down)]
    all_to_all x1 -> x0, starting transfers between devices: 15.3 us -> none  [per_device(): lax.all_to_all(parcel.astype(jnp.bfloat16), 'bcol', split_axis=0, concat_...]
  transfers between devices with their start and end apart: 11 -> 0, of which waited for: 10 -> 0; matrix products, arithmetic and copies ran while one was open for 22% -> 0% of each run, Pallas kernels for 0% -> 0%
where the time goes in v1:
time: 83.3 us; the launch traced here: 82.9 us
  Pallas kernels  80.9 us (97%)
  between operations  1.95 us (2%)
    pallas_call x1, Pallas kernels, per_device(): call(blocks_kernel, [SMEM] * 3 + [VMEM] * 3, [struct((2, NPOP, LX, 128),...  43.4 us
    pallas_call x2, Pallas kernels, halo(): call(halo_kernel, [VMEM] * 3, FACES, [sem, sem], collective_id=number, ha...  22.2 us
    pallas_call x1, Pallas kernels, per_device(): call(step_kernel, [VMEM] * 4, [FIELD] + FACES, [WIDE])(relaxed, *faces)  4.45 us
    pallas_call x1, Pallas kernels, per_device(): call(start_kernel, [SMEM] * 2 + [VMEM] * 5, [FIELD] + FACES, [pltpu.VMEM(...  4.41 us
    pallas_call x1, Pallas kernels, per_device(): call(final_kernel, [VMEM] * 4, [struct((19, LX, LANES)), struct((7, LX, L...  3.8 us
    pallas_call x1, Pallas kernels, per_device(): call(pack_kernel, [VMEM] * 4, [struct((2, NPOP, LX, 128), BF16), struct((...  2.63 us

profile of v1, /device:TPU:32, one launch (start us, length us, event | category | flops | bytes accessed | tf_op | source)
XLA Modules:
  0.0 82.9 jit_solution(16464994368549955780)
XLA Ops:
  1.9 2.6 %shard_map.95 = (bf16[2,26,16,128]{3,2,1,0:T(8,128)(2,1)}, bf16[8,64,128]{2,1,0:T(8,128)(2,1)}, bf16[8,48,128]{2,1,0:T(8,128)(2,1)}) custom-call(f32[19,16,1024]{2,1,0:T(8,128)} %hf.3, f32[7,16,1024]{2,1,0:T(8,128)} %hh.3, bf16[19,4096]{1,0:T(8,128)(2,1)} %bitcast.2, bf16[7,4096]{1,0:T(8,128)(2,1)} %bitcast.3), custom_call_target="tpu_custom_call" | custom-call | tf_op jit(solution)/shard_map/pallas_call | solution.py:625
  4.6 43.4 %shard_map.96 = (bf16[2,26,16,128]{3,2,1,0:T(8,128)(2,1)}, bf16[2,64,128]{2,1,0:T(8,128)(2,1)}, bf16[2,48,128]{2,1,0:T(8,128)(2,1)}) custom-call(s32[3,256]{1,0:T(4,128)} %constant.2.clone.table, s32[1]{0:T(128)S(6)} %copy.10.mask_ref, s32[1,1,4]{2,1,0:T(1,128)} %codes_in.3, bf16[2,26,16,128]{3,2,1,0:T(8,128)(2,1)} %get-tuple-element.22.own, ...), custom_call_target="tpu_custom_call" | custom-call | tf_op jit(solution)/shard_map/pallas_call | solution.py:632
  48.0 4.4 %shard_map.97 = (f32[26,16,1024]{2,1,0:T(8,128)}, f32[2,8,1024]{2,1,0:T(8,128)}, f32[2,3,16,128]{3,2,1,0:T(8,128)}, f32[4,8,128]{2,1,0:T(8,128)}) custom-call(s32[1,1,4]{2,1,0:T(1,128)} %codes_in.3, s32[1,1]{1,0:T(1,128)S(6)} %copy.11.moved, f32[19,16,1024]{2,1,0:T(8,128)} %hf.3, f32[7,16,1024]{2,1,0:T(8,128)} %hh.3, ...), custom_call_target="tpu_custom_call" | custom-call | tf_op jit(solution)/shard_map/pallas_call | solution.py:645
  52.4 11.1 %shard_map.98 = (f32[2,8,1024]{2,1,0:T(8,128)}, f32[2,3,16,128]{3,2,1,0:T(8,128)}, f32[4,8,128]{2,1,0:T(8,128)}) custom-call(f32[2,8,1024]{2,1,0:T(8,128)} %get-tuple-element.29.xs, f32[2,3,16,128]{3,2,1,0:T(8,128)} %get-tuple-element.30.ys, f32[4,8,128]{2,1,0:T(8,128)} %get-tuple-element.31.cs), custom_call_target="tpu_custom_call" | custom-call | tf_op jit(solution)/shard_map/pallas_call | solution.py:619
  63.5 4.4 %shard_map.99 = (f32[26,16,1024]{2,1,0:T(8,128)}, f32[2,8,1024]{2,1,0:T(8,128)}, f32[2,3,16,128]{3,2,1,0:T(8,128)}, f32[4,8,128]{2,1,0:T(8,128)}) custom-call(f32[26,16,1024]{2,1,0:T(8,128)} %get-tuple-element.28.relaxed_in, f32[2,8,1024]{2,1,0:T(8,128)} %get-tuple-element.32.xr, f32[2,3,16,128]{3,2,1,0:T(8,128)} %get-tuple-element.33.yr, ...), custom_call_target="tpu_custom_call" | custom-call | tf_op jit(solution)/shard_map/pallas_call | solution.py:651
  67.9 11.1 %shard_map.100 = (f32[2,8,1024]{2,1,0:T(8,128)}, f32[2,3,16,128]{3,2,1,0:T(8,128)}, f32[4,8,128]{2,1,0:T(8,128)}) custom-call(f32[2,8,1024]{2,1,0:T(8,128)} %get-tuple-element.36.xs, f32[2,3,16,128]{3,2,1,0:T(8,128)} %get-tuple-element.37.ys, f32[4,8,128]{2,1,0:T(8,128)} %get-tuple-element.38.cs), custom_call_target="tpu_custom_call" | custom-call | tf_op jit(solution)/shard_map/pallas_call | solution.py:619
  79.1 3.8 %shard_map.101 = (f32[19,16,1024]{2,1,0:T(8,128)}, f32[7,16,1024]{2,1,0:T(8,128)}) custom-call(f32[26,16,1024]{2,1,0:T(8,128)} %get-tuple-element.35.relaxed_in, f32[2,8,1024]{2,1,0:T(8,128)} %get-tuple-element.39.xr, f32[2,3,16,128]{3,2,1,0:T(8,128)} %get-tuple-element.40.yr, f32[4,8,128]{2,1,0:T(8,128)} %get-tuple-element.41.cr), custom_call_target="tpu_custom_call" | custom-call | tf_op jit(solution)/shard_map/pallas_call | solution.py:653

commit v2 on v1

v2 whole, which is shorter than its diff:
```python
import jax
import jax.numpy as jnp
import numpy as np
from jax import lax
from jax.experimental import pallas as pl
from jax.experimental.pallas import tpu as pltpu
from jax.sharding import PartitionSpec as P

MESH = pl.DeviceIdType.MESH
F32 = jnp.float32
BF16 = jnp.bfloat16

NPOP = 26
LX = 16
LANES = 1024
RING = 16
STEPS = 4
SPLITS = ((0, 9), (9, 18), (18, 26))
ROWS_A, ROWS_B = 64, 48

flow_cx = [0, 1, -1, 0, 0, 0, 0, 1, -1, 1, -1, 1, -1, 1, -1, 0, 0, 0, 0]
flow_cy = [0, 0, 0, 1, -1, 0, 0, 1, -1, -1, 1, 0, 0, 0, 0, 1, -1, 1, -1]
flow_cz = [0, 0, 0, 0, 0, 1, -1, 0, 0, 0, 0, 1, -1, -1, 1, 1, -1, -1, 1]
flow_weight = [1.0 / 3.0] + [1.0 / 18.0] * 6 + [1.0 / 36.0] * 12
flow_reverse = [0, 2, 1, 4, 3, 6, 5, 8, 7, 10, 9, 12, 11, 14, 13, 16, 15, 18, 17]
heat_reverse = [0, 2, 1, 4, 3, 6, 5]
POP_CX = flow_cx + flow_cx[:7]
POP_CY = flow_cy + flow_cy[:7]
POP_CZ = flow_cz + flow_cz[:7]
POP_REV = flow_reverse + [19 + r for r in heat_reverse]
X_UP = [i for i in range(NPOP) if POP_CX[i] == 1]
X_DOWN = [i for i in range(NPOP) if POP_CX[i] == -1]
Y_UP = [i for i in range(NPOP) if POP_CY[i] == 1]
Y_DOWN = [i for i in range(NPOP) if POP_CY[i] == -1]
CORNERS = ((7, 1, 1), (8, -1, -1), (9, 1, -1), (10, -1, 1))
tau_flow = 0.8
tau_heat = 0.7
tau_flow_coarse = 0.65
tau_heat_coarse = 0.6
buoyancy = 0.01
heat_ref = 7.0


def ring_jobs(mask):
    ways = ([], [])
    ties = []
    for c in range(RING):
        for h in range(2):
            start = c if mask % 2 == 0 else (c + 1 - 2 * h) % RING
            d = ((c ^ mask) - start) % RING
            if d == RING // 2:
                ties.append((d // 2, start, c, h))
            elif d:
                ways[d > RING // 2].append((min(d, RING - d) // 2, start, c, h))
    return ways, ties


def ring_seats(packets, sign):
    packets = sorted(packets, key=lambda p: (-p[0], sign * p[1] % RING, p[2], p[3]))
    busy = {}
    out = {}

    def place(n):
        if n == len(packets):
            return True
        jumps, start, c, h = packets[n]
        for t0 in range(STEPS - jumps + 1):
            taken = busy.setdefault((start - sign * 2 * t0) % RING, [])
            if all(t0 + jumps <= a or b <= t0 for a, b in taken):
                taken.append((t0, t0 + jumps))
                out[n] = t0
                if place(n + 1):
                    return True
                taken.pop()
        return False

    return [p + (out[n],) for n, p in enumerate(packets)] if place(0) else None


def ring_tables():
    word = np.zeros((RING, RING), np.int32)
    land = np.zeros((2, RING, RING), np.int32)
    for mask in range(1, RING):
        ways, ties = ring_jobs(mask)
        for pick in ((0, 1), (1, 0), (0, 0), (1, 1)):
            plan = [ring_seats(ways[w] + [p for p in ties if pick[p[3]] == w], 1 - 2 * w)
                    for w in range(2)]
            if None not in plan:
                break
        assert None not in plan
        for c in range(RING):
            for h in range(2):
                land[h, mask, c] = 2 * STEPS + h
        for w in range(2):
            for jumps, start, c, h, t0 in plan[w]:
                word[mask, start] |= (1 + h) << (2 * (w * STEPS + t0))
                land[h, mask, c ^ mask] = w * STEPS + t0 + jumps - 1
    return np.stack([word.reshape(-1), land[0].reshape(-1), land[1].reshape(-1)])


RING_TABLE = ring_tables()


def lane_ids(rows):
    return lax.broadcasted_iota(jnp.int32, (rows, 128), 1)


def total(values):
    values = list(values)
    while len(values) > 1:
        values = [a + b for a, b in zip(values[::2], values[1::2])] + (
            [values[-1]] if len(values) % 2 else [])
    return values[0]


def moments(f, push):
    rho = total(f[:19])
    heat = total(f[19:])

    def along(c):
        ups = [f[i] for i in range(19) if c[i] == 1]
        downs = [f[i] for i in range(19) if c[i] == -1]
        return total([u - d for u, d in zip(ups, downs)])

    mx, my, mz = along(flow_cx), along(flow_cy), along(flow_cz)
    force = None
    if push:
        force = buoyancy * rho * (heat - heat_ref)
        mz = mz + 0.5 * force
    inv = 1.0 / rho
    return rho, heat, force, (mx, my, mz), (mx * inv, my * inv, mz * inv)


def dot_dir(i, v):
    terms = []
    for c, a in zip((flow_cx[i], flow_cy[i], flow_cz[i]), v):
        if c:
            terms.append((c, a))
    out = terms[0][1] if terms[0][0] > 0 else -terms[0][1]
    for c, a in terms[1:]:
        out = out + a if c > 0 else out - a
    return out


PAIRS = [(1, 2), (3, 4), (5, 6), (7, 8), (9, 10), (11, 12), (13, 14), (15, 16), (17, 18)]


def collide(f):
    rho, heat, force, mom, vel = moments(f, True)
    rate = 1.0 / tau_flow
    keep = 1.0 - rate
    gain = 1.0 - 0.5 / tau_flow
    speed = mom[0] * vel[0] + mom[1] * vel[1] + mom[2] * vel[2]
    common = rate * rho - (1.5 * rate) * speed - (3.0 * gain) * force * vel[2]
    fgain = (9.0 * gain) * force
    fodd = (3.0 * gain) * force
    out = [None] * NPOP
    out[0] = keep * f[0] + flow_weight[0] * common
    for i, j in PAIRS:
        w = flow_weight[i]
        cu = dot_dir(i, vel)
        cm = dot_dir(i, mom)
        bracket = (4.5 * rate) * cm
        odd = (3.0 * rate) * cm
        if flow_cz[i] == 1:
            bracket = bracket + fgain
            odd = odd + fodd
        elif flow_cz[i] == -1:
            bracket = bracket - fgain
            odd = odd - fodd
        even = common + bracket * cu
        out[i] = keep * f[i] + w * (even + odd)
        out[j] = keep * f[j] + w * (even - odd)
    hrate = 1.0 / tau_heat
    hkeep = 1.0 - hrate
    out[19] = hkeep * f[19] + (0.25 * hrate) * heat
    side = (0.125 * hrate) * heat
    for k, a in zip((20, 22, 24), vel):
        tilt = 4.0 * side * a
        out[k] = hkeep * f[k] + (side + tilt)
        out[k + 1] = hkeep * f[k + 1] + (side - tilt)
    return out


def explode(f):
    rho, heat, _, mom, vel = moments(f, False)
    blend = tau_flow / (2.0 * tau_flow_coarse)
    rest = 1.0 - blend
    speed = mom[0] * vel[0] + mom[1] * vel[1] + mom[2] * vel[2]
    common = rest * rho - (1.5 * rest) * speed
    out = [None] * NPOP
    out[0] = blend * f[0] + flow_weight[0] * common
    for i, j in PAIRS:
        w = flow_weight[i]
        cu = dot_dir(i, vel)
        cm = dot_dir(i, mom)
        even = common + ((4.5 * rest) * cm) * cu
        odd = (3.0 * rest) * cm
        out[i] = blend * f[i] + w * (even + odd)
        out[j] = blend * f[j] + w * (even - odd)
    hblend = tau_heat / (2.0 * tau_heat_coarse)
    hrest = 1.0 - hblend
    out[19] = hblend * f[19] + (0.25 * hrest) * heat
    side = (0.125 * hrest) * heat
    for k, a in zip((20, 22, 24), vel):
        tilt = 4.0 * side * a
        out[k] = hblend * f[k] + (side + tilt)
        out[k + 1] = hblend * f[k + 1] + (side - tilt)
    return out


def held_tile(hf, hh, p, rows, cols):
    return hf[p, rows, cols] if p < 19 else hh[p - 19, rows, cols]


def pack_trade(hf, hh, own):
    group = lane_ids(LX) % 64 // 16
    for p in range(NPOP):
        for q in range(2):
            packed = None
            for kk in range(4):
                k = 4 * q + kk
                tile = held_tile(hf, hh, p, slice(None), slice(128 * k, 128 * k + 128))
                if kk == 0:
                    packed = tile
                else:
                    packed = jnp.where(group == kk, pltpu.roll(tile, 16 * kk, 1), packed)
            own[q, p] = packed.astype(BF16)


def pack_coarse(cf, ch, spread, put):
    for t in range(32):
        cols = slice(128 * t, 128 * t + 128)
        flow = cf[:, cols].astype(F32)
        heat = ch[:, cols].astype(F32)
        spread[pl.ds(t, 8, stride=32), :] = flow[0:8]
        spread[pl.ds(8 * 32 + t, 8, stride=32), :] = flow[8:16]
        spread[pl.ds(16 * 32 + t, 3, stride=32), :] = flow[16:19]
        spread[pl.ds(19 * 32 + t, 7, stride=32), :] = heat
    high = lane_ids(8) // 8 % 2 == 1
    zeros = jnp.zeros((8, 128), F32)
    for ox in range(2):
        for oy in range(2):
            low_rows, high_rows = [], []
            for pair in range(13):
                a = spread[pl.ds(pair * 32 + 16 * ox + oy, 8, stride=2), :]
                b = spread[pl.ds((pair + 13) * 32 + 16 * ox + oy, 8, stride=2), :]
                low_rows.append(jnp.where(high, pltpu.roll(b, 8, 1), a))
                high_rows.append(jnp.where(high, b, pltpu.roll(a, 120, 1)))
            for oz, rows in ((0, low_rows), (1, high_rows)):
                rows = rows + [zeros]
                for i in range(7):
                    put(4 * ox + 2 * oy + oz, i,
                        jnp.concatenate([rows[2 * i], rows[2 * i + 1]], axis=0).astype(BF16))


def place():
    me = lax.axis_index("brow")
    col = lax.axis_index("bcol")
    return me // 8, me // 2 % 4, me % 2, col


def row_of(x, y, k):
    return (x * 4 + y) * 2 + k


OFFSETS = [(d, dk) for d in range(4) for dk in range(2)]


OFFSETS = [(d, dk) for d in range(4) for dk in range(2)]


def edge_faces(field, xs, ys, cs, base, lead):
    low = lane_ids(LX) < 64
    for n, p in enumerate(X_UP):
        xs[0, n:n + 1, :] = field[p, base + 15:base + 16, lead:lead + LANES]
    for n, p in enumerate(X_DOWN):
        xs[1, n:n + 1, :] = field[p, base:base + 1, lead:lead + LANES]
    rows = slice(base, base + LX)
    last = slice(lead + LANES - 128, lead + LANES)
    first = slice(lead, lead + 128)
    for n in range(3):
        a, b = Y_UP[2 * n], Y_UP[2 * n + 1]
        ys[0, n] = jnp.where(low, pltpu.roll(field[a, rows, last], 64, 1), field[b, rows, last])
        a, b = Y_DOWN[2 * n], Y_DOWN[2 * n + 1]
        ys[1, n] = jnp.where(low, field[a, rows, first], pltpu.roll(field[b, rows, first], 64, 1))
    for n, (p, sx, sy) in enumerate(CORNERS):
        cs[n] = field[p, base + 8:base + 16, last] if (sx, sy) == (1, 1) else (
            field[p, base:base + 8, first] if (sx, sy) == (-1, -1) else (
                field[p, base + 8:base + 16, first] if (sx, sy) == (1, -1) else
                field[p, base:base + 8, last]))


def widen(relaxed, xr, yr, cr, wide):
    for p in range(NPOP):
        wide[p, 8:24, 128:128 + LANES] = relaxed[p]
    fill_edges(xr, yr, cr, wide)


def fill_edges(xr, yr, cr, wide):
    for n, (p, sx, sy) in enumerate(CORNERS):
        rows = slice(0, 8) if sx == 1 else slice(24, 32)
        cols = slice(0, 128) if sy == 1 else slice(128 + LANES, 256 + LANES)
        wide[p, rows, cols] = cr[n]
    for n, p in enumerate(X_UP):
        wide[p, 7:8, 128:128 + LANES] = xr[0, n:n + 1, :]
    for n, p in enumerate(X_DOWN):
        wide[p, 24:25, 128:128 + LANES] = xr[1, n:n + 1, :]
    for n in range(3):
        a, b = Y_UP[2 * n], Y_UP[2 * n + 1]
        wide[a, 8:24, 0:128] = pltpu.roll(yr[0, n], 64, 1)
        wide[b, 8:24, 0:128] = yr[0, n]
        a, b = Y_DOWN[2 * n], Y_DOWN[2 * n + 1]
        wide[a, 8:24, 128 + LANES:256 + LANES] = yr[1, n]
        wide[b, 8:24, 128 + LANES:256 + LANES] = pltpu.roll(yr[1, n], 64, 1)


def pulled(wide, p, rt, k):
    cx, cy, cz = POP_CX[p], POP_CY[p], POP_CZ[p]
    rows = slice(8 + 8 * rt - cx, 16 + 8 * rt - cx)

    def tile(e):
        return pl.ds(pl.multiple_of(128 * e, 128), 128)

    low = lane_ids(8) < 64
    value = wide[p, rows, tile(k + 1)]
    shift = 0
    if cy == 1:
        value = jnp.where(low, value, wide[p, rows, tile(k)])
        shift = 64
    elif cy == -1:
        value = jnp.where(low, wide[p, rows, tile(k + 2)], value)
        shift = 64
    shift = (shift + cz) % 128
    if shift:
        value = pltpu.roll(value, shift, 1)
    if cz:
        wall = lane_ids(8) % 64 == (0 if cz == 1 else 63)
        back = wide[POP_REV[p], 8 + 8 * rt:16 + 8 * rt, tile(k + 1)]
        value = jnp.where(wall, back, value)
    return value


def by_slot(lane, picks):
    slot = lane % 64 // 16
    return jnp.where(slot == 0, picks[0], jnp.where(
        slot == 1, picks[1], jnp.where(slot == 2, picks[2], picks[3])))


def first_and_last(values):
    first, last = values[3], values[0]
    for j in (2, 1, 0):
        first = jnp.where(values[j] >= 0, values[j], first)
    for j in (1, 2, 3):
        last = jnp.where(values[j] >= 0, values[j], last)
    return first, last


def one_hots(children, trades, child, trade):
    for t in range(8):
        lane = lax.broadcasted_iota(jnp.int32, (1, 128), 1)
        yy = 2 * t + lane // 64
        want = yy // 2 * 16 + lane % 16 // 2 + by_slot(lane, child)
        row = lax.broadcasted_iota(jnp.int32, (128, 128), 0)
        hot = jnp.where(row == want, 1.0, 0.0).astype(BF16)
        cols = slice(128 * t, 128 * t + 128)
        children[0:128, cols] = hot
        children[128:256, cols] = hot
        row = lax.broadcasted_iota(jnp.int32, (256, 128), 0)
        z = lane % 64
        want = yy // 8 * 128 + yy % 2 * 64 + yy % 8 // 2 * 16 + z
        want = jnp.where(z < 16, want + trade, 1 << 20)
        trades[:, cols] = jnp.where(row == want, 1.0, 0.0).astype(BF16)


def refine(picked_a, picked_b, spread, left):
    high = lane_ids(8) // 8 % 2 == 1
    values = [None] * NPOP
    for pair in range(13):
        part, row = (picked_a, 8 * pair) if pair < 8 else (picked_b, 8 * pair - 64)
        base = row // 16 * 16
        a = part[0, base:base + 16, :].astype(F32)[row - base:row - base + 8]
        b = part[1, base:base + 16, :].astype(F32)[row - base:row - base + 8]
        values[pair] = jnp.where(high, pltpu.roll(b, 8, 1), a)
        values[pair + 13] = jnp.where(high, b, pltpu.roll(a, 120, 1))
    for p, value in enumerate(explode(values)):
        spread[pl.ds(16 * p, 8, stride=2), :] = value
        spread[pl.ds(16 * p + 1, 8, stride=2), :] = value
    for p in range(NPOP):
        rows = slice(16 * p, 16 * p + 16)
        value = spread[rows, :]
        top = value.astype(BF16)
        left[rows, 0:128] = top
        left[rows, 128:256] = (value - top.astype(F32)).astype(BF16)


def main_kernel(table, mask_ref, moved, codes_in, hf, hh, cf, ch,
                relaxed, xr2, yr2, cr2,
                own, landing, leaving, ready, held_a, held_b, codes,
                stage_a, stage_b, got_a, got_b, picked_a, picked_b,
                spread, left, children, trades, fresh, wide,
                xs1, ys1, cs1, xr1, yr1, cr1, xs2, ys2, cs2,
                ring_send, ring_recv, code_send, code_recv, one_send, one_recv,
                two_send, two_recv, halo_send, halo_recv):
    x, y, k, col = place()
    me = row_of(x, y, k)
    x_group = [row_of(x, (y + d) % 4, (k + dk) % 2) for d, dk in OFFSETS]
    y_group = [row_of((x + d) % 4, y, (k + dk) % 2) for d, dk in OFFSETS]
    peers = x_group[1:] + y_group[2:]
    near_row = {1: (me + 1) % 32, -1: (me + 31) % 32, 0: me}
    near_col = {d: (col + d + RING) % RING for d in (-2, -1, 0, 1, 2)}

    barrier = pltpu.get_barrier_semaphore()
    greeted = [(me, near_col[d]) for d in (-2, -1, 1, 2)] + [(peer, col) for peer in peers]
    greeted += [(near_row[sx], near_col[sy]) for sx in (-1, 1) for sy in (-1, 0, 1)]
    for device in greeted:
        pl.semaphore_signal(barrier, inc=1, device_id=device, device_id_type=MESH)

    pending = []

    def send(source, target, sends, recvs, device):
        copy = pltpu.make_async_remote_copy(
            src_ref=source, dst_ref=target, send_sem=sends, recv_sem=recvs,
            device_id=device, device_id_type=MESH)
        copy.start()
        pending.append(copy)
        return copy

    entry = mask_ref[0] * RING + col
    word = table[0, entry]
    odd = mask_ref[0] & 1
    ring = {}

    def ring_send_slot(source, slot, s, device):
        lo, hi = SPLITS[s]
        ring[slot, s] = send(source.at[lo:hi], landing.at[slot, lo:hi],
                             ring_send.at[slot, s], ring_recv.at[slot, s], device)

    def ring_step(step):
        for s, (lo, hi) in enumerate(SPLITS):
            if step == 0:
                for h in range(2):
                    ring[2 * STEPS + h, s].wait_recv()
                    ready[h, lo:hi] = jnp.where(odd == 1, landing[2 * STEPS + h, lo:hi],
                                                own[h, lo:hi])
            for way in range(2):
                slot = way * STEPS + step
                code = (word >> (2 * slot)) & 3
                other = ready[0, lo:hi]
                if step:
                    ring[slot - 1, s].wait_recv()
                    other = jnp.where(code == 1, other, landing[slot - 1, lo:hi])
                leaving[slot, lo:hi] = jnp.where(code == 2, ready[1, lo:hi], other)
                ring_send_slot(leaving.at[slot], slot, s, (me, near_col[2 - 4 * way]))

    pack_trade(hf, hh, own)
    pl.semaphore_wait(barrier, len(greeted))
    for s in range(len(SPLITS)):
        for h in range(2):
            ring_send_slot(own.at[h], 2 * STEPS + h, s, (me, near_col[1 - 2 * h]))
    code_copies = [send(codes_in, codes.at[n], code_send.at[n], code_recv.at[n], (peer, col))
                   for n, peer in enumerate(peers)]

    def put(octant, i, value):
        if i < 4:
            held_a[0, octant, 16 * i:16 * i + 16, :] = value
        else:
            held_b[0, octant, 16 * (i - 4):16 * (i - 4) + 16, :] = value

    pack_coarse(cf, ch, spread, put)
    one_copies = []
    for d in (2, 1, 3):
        one_copies.append(send(held_a.at[0], held_a.at[d], one_send.at[0, d], one_recv.at[0, d],
                               (row_of((x + d) % 4, y, k), col)))
        one_copies.append(send(held_b.at[0], held_b.at[d], one_send.at[1, d], one_recv.at[1, d],
                               (row_of(x, (y + d) % 4, k), col)))
    ring_step(0)

    source = [codes_in[0, 0, j] for j in range(4)]
    refined = [jnp.where(v >= 0, 1, 0) for v in source]
    rank = [0]
    for j in range(3):
        rank.append(rank[-1] + refined[j])
    child = [jnp.where(refined[j] == 1, rank[j] * 8, 1 << 20) for j in range(4)]
    trade = jnp.where((moved[0, 0] > 0) & (refined[0] == 0), 0, 1 << 20)
    one_hots(children, trades, child, trade)
    ring_step(1)

    for copy in code_copies + one_copies:
        copy.wait_recv()
    mine = first_and_last(source)
    two_copies = []
    for n, (d, dk) in enumerate(OFFSETS):
        for part, (group, stage, got, held, home) in enumerate((
                (x_group, stage_a, got_a, held_a, x), (y_group, stage_b, got_b, held_b, y))):
            if n == 0:
                pair = mine
            else:
                back = OFFSETS.index(((4 - d) % 4, dk))
                row = back - 1 if part == 0 or d == 0 else 7 + back - 2
                pair = first_and_last([codes[row, 0, 0, j] for j in range(4)])
            for s, code in enumerate(pair):
                parent = (code >> 6) & 3 if part == 0 else (code >> 4) & 3
                value = held[(home - parent + 4) & 3, code & 7]
                if n == 0:
                    got[0, s] = value
                else:
                    stage[n, s] = value
            if n:
                two_copies.append(send(stage.at[n], got.at[n], two_send.at[part, n],
                                       two_recv.at[part, n], (group[n], col)))
    ring_step(2)
    ring_step(3)

    for copy in two_copies:
        copy.wait_recv()
    for s, code in enumerate(mine):
        core = ((code >> 3) & 1) ^ k
        picked_a[s] = got_a[((y - ((code >> 4) & 3) + 4) & 3) * 2 + core, s]
        picked_b[s] = got_b[((x - ((code >> 6) & 3) + 4) & 3) * 2 + core, s]
    refine(picked_a, picked_b, spread, left)
    for t in range(4):
        cols = slice(256 * t, 256 * t + 256)
        fresh[:, cols] = jnp.dot(left[...], children[:, cols], preferred_element_type=F32)
    keep = [1 - refined[j] for j in range(4)]
    keep[0] = jnp.where(moved[0, 0] > 0, 0, keep[0])
    kept = by_slot(lane_ids(8), keep) == 1

    def merge(t, carry):
        cols = pl.ds(pl.multiple_of(128 * t, 128), 128)
        for p in range(NPOP):
            for rt in range(2):
                rows = slice(16 * p + 8 * rt, 16 * p + 8 * rt + 8)
                fresh[rows, cols] = jnp.where(
                    kept, held_tile(hf, hh, p, slice(8 * rt, 8 * rt + 8), cols),
                    fresh[rows, cols])
        return carry

    lax.fori_loop(0, 8, merge, 0)

    for way in range(2):
        for s in range(len(SPLITS)):
            ring[way * STEPS + STEPS - 1, s].wait_recv()
    for h in range(2):
        left[:, 128 * h:128 * h + 128] = landing[table[1 + h, entry]].reshape(NPOP * LX, 128)
    for t in range(4):
        cols = slice(256 * t, 256 * t + 256)
        fresh[:, cols] += jnp.dot(left[...], trades[:, cols], preferred_element_type=F32)

    def exchange(turn, faces, arrivals):
        (xs, ys, cs), (xr, yr, cr) = faces, arrivals
        moves = [(cs.at[n], cr.at[n], sx, sy) for n, (p, sx, sy) in enumerate(CORNERS)]
        moves += [(xs.at[0], xr.at[0], 1, 0), (xs.at[1], xr.at[1], -1, 0),
                  (ys.at[0], yr.at[0], 0, 1), (ys.at[1], yr.at[1], 0, -1)]
        return [send(a, b, halo_send.at[turn, n], halo_recv.at[turn, n],
                     (near_row[sx], near_col[sy])) for n, (a, b, sx, sy) in enumerate(moves)]

    def first_step(t, carry):
        cols = pl.ds(pl.multiple_of(128 * t, 128), 128)
        wide_cols = pl.ds(pl.multiple_of(128 * t + 128, 128), 128)
        for rt in range(2):
            f = [fresh[16 * p + 8 * rt:16 * p + 8 * rt + 8, cols] for p in range(NPOP)]
            for p, value in enumerate(collide(f)):
                wide[p, 8 + 8 * rt:16 + 8 * rt, wide_cols] = value
        return carry

    lax.fori_loop(0, 8, first_step, 0)
    edge_faces(wide, xs1, ys1, cs1, 8, 128)
    for copy in exchange(0, (xs1, ys1, cs1), (xr1, yr1, cr1)):
        copy.wait_recv()
    fill_edges(xr1, yr1, cr1, wide)

    def second_step(t, carry):
        cols = pl.ds(pl.multiple_of(128 * t, 128), 128)
        for rt in range(2):
            f = [pulled(wide, p, rt, t) for p in range(NPOP)]
            for p, value in enumerate(collide(f)):
                relaxed[p, 8 * rt:8 * rt + 8, cols] = value
        return carry

    lax.fori_loop(0, 8, second_step, 0)
    edge_faces(relaxed, xs2, ys2, cs2, 0, 0)
    for copy in exchange(1, (xs2, ys2, cs2), (xr2, yr2, cr2)):
        copy.wait_recv()
    for copy in pending:
        copy.wait_send()


def final_kernel(relaxed_in, xr, yr, cr, out_flow, out_heat, wide):
    widen(relaxed_in, xr, yr, cr, wide)

    def body(k, carry):
        cols = pl.ds(pl.multiple_of(128 * k, 128), 128)
        for rt in range(2):
            for p in range(NPOP):
                value = pulled(wide, p, rt, k)
                if p < 19:
                    out_flow[p, 8 * rt:8 * rt + 8, cols] = value
                else:
                    out_heat[p - 19, 8 * rt:8 * rt + 8, cols] = value
        return carry

    lax.fori_loop(0, 8, body, 0)


VMEM = pl.BlockSpec(memory_space=pltpu.VMEM)
SMEM = pl.BlockSpec(memory_space=pltpu.SMEM)


def struct(shape, dtype=F32):
    return jax.ShapeDtypeStruct(shape, dtype)


FACES = [struct((2, 8, LANES)), struct((2, 3, LX, 128)), struct((4, 8, 128))]
FIELD = struct((NPOP, LX, LANES))
WIDE = pltpu.VMEM((NPOP, 32, LANES + 256), F32)


def call(kernel, ins, outs, scratch, **params):
    return pl.pallas_call(
        kernel, out_shape=outs, in_specs=ins,
        out_specs=jax.tree.map(lambda _: VMEM, outs), scratch_shapes=scratch,
        compiler_params=pltpu.CompilerParams(vmem_limit_bytes=56 * 2**20, **params))


def vmem(spec):
    return pltpu.VMEM(spec.shape, spec.dtype)


def per_device(held_flow, held_heat, coarse_flow, coarse_heat, pair_mask, moved_count, refine_src):
    dma = pltpu.SemaphoreType.DMA
    ns = len(SPLITS)
    slots = 2 * STEPS + 2
    block = (NPOP, LX, 128)
    relaxed, *faces = call(
        main_kernel, [SMEM] * 4 + [VMEM] * 4, [FIELD] + FACES,
        [pltpu.VMEM((2,) + block, BF16), pltpu.VMEM((slots,) + block, BF16),
         pltpu.VMEM((2 * STEPS,) + block, BF16), pltpu.VMEM((2,) + block, BF16),
         pltpu.VMEM((4, 8, ROWS_A, 128), BF16), pltpu.VMEM((4, 8, ROWS_B, 128), BF16),
         pltpu.SMEM((13, 1, 1, 4), jnp.int32),
         pltpu.VMEM((8, 2, ROWS_A, 128), BF16), pltpu.VMEM((8, 2, ROWS_B, 128), BF16),
         pltpu.VMEM((8, 2, ROWS_A, 128), BF16), pltpu.VMEM((8, 2, ROWS_B, 128), BF16),
         pltpu.VMEM((2, ROWS_A, 128), BF16), pltpu.VMEM((2, ROWS_B, 128), BF16),
         pltpu.VMEM((NPOP * 32, 128), F32), pltpu.VMEM((NPOP * LX, 256), BF16),
         pltpu.VMEM((256, LANES), BF16), pltpu.VMEM((256, LANES), BF16),
         pltpu.VMEM((NPOP * LX, LANES), F32), WIDE]
        + [vmem(f) for f in FACES * 3]
        + [dma((slots, ns)), dma((slots, ns)), dma((13,)), dma((13,)),
           dma((2, 4)), dma((2, 4)), dma((2, 8)), dma((2, 8)), dma((2, 8)), dma((2, 8))],
        collective_id=0, has_side_effects=True)(
            jnp.asarray(RING_TABLE), pair_mask, moved_count, refine_src,
            held_flow, held_heat, coarse_flow.reshape(19, 4096), coarse_heat.reshape(7, 4096))
    return tuple(call(final_kernel, [VMEM] * 4,
                      [struct((19, LX, LANES)), struct((7, LX, LANES))], [WIDE])(relaxed, *faces))


def solution(mesh):
    return jax.shard_map(
        per_device,
        mesh=mesh,
        in_specs=(
            P(None, "brow", "bcol"),
            P(None, "brow", "bcol"),
            P(None, "brow", "bcol", None),
            P(None, "brow", "bcol", None),
            P("brow"),
            P("brow", "bcol"),
            P("brow", "bcol", None),
        ),
        out_specs=(P(None, "brow", "bcol"), P(None, "brow", "bcol")),
        check_vma=False,
    )
```

time: 83.3 us -> 62 us (0.74)
  Pallas kernels: 80.9 us -> 59.9 us
    pallas_call x6 -> x1, Pallas kernels: 77.1 us -> 56.1 us  [per_device(): call(main_kernel, [SMEM] * 4 + [VMEM] * 4, [FIELD] + FACES, [pltpu.VMEM((...]
where the time goes in v2:
time: 62 us; the launch traced here: 61.9 us
  Pallas kernels  59.9 us (97%)
  between operations  1.93 us (3%)
    pallas_call x1, Pallas kernels, per_device(): call(main_kernel, [SMEM] * 4 + [VMEM] * 4, [FIELD] + FACES, [pltpu.VMEM((...  56.1 us
    pallas_call x1, Pallas kernels, per_device(): call(final_kernel, [VMEM] * 4, [struct((19, LX, LANES)), struct((7, LX, L...  3.8 us

profile of v2, /device:TPU:32, one launch (start us, length us, event | category | flops | bytes accessed | tf_op | source)
XLA Modules:
  0.0 61.9 jit_solution(3493333589218669026)
XLA Ops:
  1.9 56.1 %shard_map.95 = (f32[26,16,1024]{2,1,0:T(8,128)}, f32[2,8,1024]{2,1,0:T(8,128)}, f32[2,3,16,128]{3,2,1,0:T(8,128)}, f32[4,8,128]{2,1,0:T(8,128)}) custom-call(s32[3,256]{1,0:T(4,128)} %constant.2.clone.table, s32[1]{0:T(128)S(6)} %copy.10.mask_ref, s32[1,1]{1,0:T(1,128)S(6)} %copy.11.moved, s32[1,1,4]{2,1,0:T(1,128)} %codes_in.1, f32[19,16,1024]{2,1,0:T(8,128)} %hf.1, ...), custom_call_target="tpu_custom_call" | custom-call | tf_op jit(solution)/shard_map/pallas_call | solution.py:635
  58.1 3.8 %shard_map.96 = (f32[19,16,1024]{2,1,0:T(8,128)}, f32[7,16,1024]{2,1,0:T(8,128)}) custom-call(f32[26,16,1024]{2,1,0:T(8,128)} %get-tuple-element.6.relaxed_in, f32[2,8,1024]{2,1,0:T(8,128)} %get-tuple-element.7.xr, f32[2,3,16,128]{3,2,1,0:T(8,128)} %get-tuple-element.8.yr, f32[4,8,128]{2,1,0:T(8,128)} %get-tuple-element.9.cr), custom_call_target="tpu_custom_call" | custom-call | tf_op jit(solution)/shard_map/pallas_call | solution.py:653

commit v3 on v2

--- a/solution.py
+++ b/solution.py
@@ -14,7 +14,8 @@
 LX = 16
 LANES = 1024
 RING = 16
-STEPS = 4
+JUMPS = (1, 2, 2, 2, 1)
+STEPS = len(JUMPS)
 SPLITS = ((0, 9), (9, 18), (18, 26))
 ROWS_A, ROWS_B = 64, 48
 
@@ -41,64 +42,65 @@
 heat_ref = 7.0
 
 
-def ring_jobs(mask):
-    ways = ([], [])
-    ties = []
+def ring_plan(mask):
+    travels = {d: [] for d in range(RING // 2 + 1)}
+    for picks in range(1 << STEPS):
+        steps = tuple(t for t in range(STEPS) if picks >> t & 1)
+        travels.setdefault(sum(JUMPS[t] for t in steps), []).append(steps)
+    for d in travels:
+        travels[d].sort(key=lambda steps: (len(steps), steps))
+    packets = []
     for c in range(RING):
+        d = ((c ^ mask) - c) % RING
         for h in range(2):
-            start = c if mask % 2 == 0 else (c + 1 - 2 * h) % RING
-            d = ((c ^ mask) - start) % RING
-            if d == RING // 2:
-                ties.append((d // 2, start, c, h))
-            elif d:
-                ways[d > RING // 2].append((min(d, RING - d) // 2, start, c, h))
-    return ways, ties
-
-
-def ring_seats(packets, sign):
-    packets = sorted(packets, key=lambda p: (-p[0], sign * p[1] % RING, p[2], p[3]))
-    busy = {}
-    out = {}
-
-    def place(n):
-        if n == len(packets):
+            way = h if 2 * d == RING else int(2 * d > RING)
+            packets.append((c, h, way, travels[min(d, RING - d)]))
+    used = set()
+    plan = {}
+
+    def copies(c, way, steps):
+        out = []
+        for t in steps:
+            out.append((way, t, c))
+            c = (c + (1 - 2 * way) * JUMPS[t]) % RING
+        return out
+
+    def place(left):
+        if not left:
             return True
-        jumps, start, c, h = packets[n]
-        for t0 in range(STEPS - jumps + 1):
-            taken = busy.setdefault((start - sign * 2 * t0) % RING, [])
-            if all(t0 + jumps <= a or b <= t0 for a, b in taken):
-                taken.append((t0, t0 + jumps))
-                out[n] = t0
-                if place(n + 1):
-                    return True
-                taken.pop()
+        fits = [[steps for steps in p[3] if used.isdisjoint(copies(p[0], p[2], steps))]
+                for p in left]
+        n = min(range(len(left)), key=lambda i: len(fits[i]))
+        c, h, way, _ = left[n]
+        for steps in fits[n]:
+            taken = copies(c, way, steps)
+            used.update(taken)
+            plan[c, h] = (way, steps, taken)
+            if place(left[:n] + left[n + 1:]):
+                return True
+            used.difference_update(taken)
         return False
 
-    return [p + (out[n],) for n, p in enumerate(packets)] if place(0) else None
+    assert place(packets)
+    return plan
 
 
 def ring_tables():
-    word = np.zeros((RING, RING), np.int32)
+    code = np.zeros((RING, RING, 2 * STEPS), np.int32)
     land = np.zeros((2, RING, RING), np.int32)
     for mask in range(1, RING):
-        ways, ties = ring_jobs(mask)
-        for pick in ((0, 1), (1, 0), (0, 0), (1, 1)):
-            plan = [ring_seats(ways[w] + [p for p in ties if pick[p[3]] == w], 1 - 2 * w)
-                    for w in range(2)]
-            if None not in plan:
-                break
-        assert None not in plan
-        for c in range(RING):
-            for h in range(2):
-                land[h, mask, c] = 2 * STEPS + h
-        for w in range(2):
-            for jumps, start, c, h, t0 in plan[w]:
-                word[mask, start] |= (1 + h) << (2 * (w * STEPS + t0))
-                land[h, mask, c ^ mask] = w * STEPS + t0 + jumps - 1
-    return np.stack([word.reshape(-1), land[0].reshape(-1), land[1].reshape(-1)])
-
-
-RING_TABLE = ring_tables()
+        for (c, h), (way, steps, taken) in ring_plan(mask).items():
+            source = h
+            for _, t, node in taken:
+                code[mask, node, way * STEPS + t] = source
+                source = 2 + t
+            land[h, mask, c ^ mask] = way * STEPS + steps[-1]
+    word = sum(code[:, :, n] << (3 * n) for n in range(2 * STEPS))
+    kinds = [sorted(set(code[:, :, n].reshape(-1).tolist())) for n in range(2 * STEPS)]
+    return np.stack([word.reshape(-1), land[0].reshape(-1), land[1].reshape(-1)]), kinds
+
+
+RING_TABLE, RING_KINDS = ring_tables()
 
 
 def lane_ids(rows):
@@ -209,22 +211,15 @@
     return out
 
 
-def held_tile(hf, hh, p, rows, cols):
-    return hf[p, rows, cols] if p < 19 else hh[p - 19, rows, cols]
-
-
-def pack_trade(hf, hh, own):
+def pack_trade(held, own, lo, hi):
     group = lane_ids(LX) % 64 // 16
-    for p in range(NPOP):
+    for p in range(lo, hi):
         for q in range(2):
-            packed = None
-            for kk in range(4):
+            packed = held[p, :, 512 * q:512 * q + 128]
+            for kk in range(1, 4):
                 k = 4 * q + kk
-                tile = held_tile(hf, hh, p, slice(None), slice(128 * k, 128 * k + 128))
-                if kk == 0:
-                    packed = tile
-                else:
-                    packed = jnp.where(group == kk, pltpu.roll(tile, 16 * kk, 1), packed)
+                tile = held[p, :, 128 * k:128 * k + 128]
+                packed = jnp.where(group == kk, pltpu.roll(tile, 16 * kk, 1), packed)
             own[q, p] = packed.astype(BF16)
 
 
@@ -270,31 +265,26 @@
 OFFSETS = [(d, dk) for d in range(4) for dk in range(2)]
 
 
-def edge_faces(field, xs, ys, cs, base, lead):
-    low = lane_ids(LX) < 64
+def x_faces(field, xs, base, lead):
     for n, p in enumerate(X_UP):
         xs[0, n:n + 1, :] = field[p, base + 15:base + 16, lead:lead + LANES]
     for n, p in enumerate(X_DOWN):
         xs[1, n:n + 1, :] = field[p, base:base + 1, lead:lead + LANES]
+
+
+def y_faces(field, ys, cs, base, lead):
+    low = lane_ids(LX) < 64
     rows = slice(base, base + LX)
     last = slice(lead + LANES - 128, lead + LANES)
     first = slice(lead, lead + 128)
+    for n, (p, sx, sy) in enumerate(CORNERS):
+        top = base + 8 if sx == 1 else base
+        cs[n] = field[p, top:top + 8, last if sy == 1 else first]
     for n in range(3):
         a, b = Y_UP[2 * n], Y_UP[2 * n + 1]
         ys[0, n] = jnp.where(low, pltpu.roll(field[a, rows, last], 64, 1), field[b, rows, last])
         a, b = Y_DOWN[2 * n], Y_DOWN[2 * n + 1]
         ys[1, n] = jnp.where(low, field[a, rows, first], pltpu.roll(field[b, rows, first], 64, 1))
-    for n, (p, sx, sy) in enumerate(CORNERS):
-        cs[n] = field[p, base + 8:base + 16, last] if (sx, sy) == (1, 1) else (
-            field[p, base:base + 8, first] if (sx, sy) == (-1, -1) else (
-                field[p, base + 8:base + 16, first] if (sx, sy) == (1, -1) else
-                field[p, base:base + 8, last]))
-
-
-def widen(relaxed, xr, yr, cr, wide):
-    for p in range(NPOP):
-        wide[p, 8:24, 128:128 + LANES] = relaxed[p]
-    fill_edges(xr, yr, cr, wide)
 
 
 def fill_edges(xr, yr, cr, wide):
@@ -320,6 +310,8 @@
     rows = slice(8 + 8 * rt - cx, 16 + 8 * rt - cx)
 
     def tile(e):
+        if isinstance(e, int):
+            return slice(128 * e, 128 * e + 128)
         return pl.ds(pl.multiple_of(128 * e, 128), 128)
 
     low = lane_ids(8) < 64
@@ -395,14 +387,23 @@
 
 
 def main_kernel(table, mask_ref, moved, codes_in, hf, hh, cf, ch,
-                relaxed, xr2, yr2, cr2,
-                own, landing, leaving, ready, held_a, held_b, codes,
+                relaxed_out, xr2, yr2, cr2,
+                held, cfv, chv, relaxed, own, landing, leaving, held_a, held_b, codes,
                 stage_a, stage_b, got_a, got_b, picked_a, picked_b,
                 spread, left, children, trades, fresh, wide,
                 xs1, ys1, cs1, xr1, yr1, cr1, xs2, ys2, cs2,
                 ring_send, ring_recv, code_send, code_recv, one_send, one_recv,
-                two_send, two_recv, halo_send, halo_recv):
+                two_send, two_recv, halo_send, halo_recv, local):
     x, y, k, col = place()
+    loads = [[pltpu.make_async_copy(hf.at[0:9], held.at[0:9], local.at[0])],
+             [pltpu.make_async_copy(hf.at[9:18], held.at[9:18], local.at[1])],
+             [pltpu.make_async_copy(hf.at[18:19], held.at[18:19], local.at[2]),
+              pltpu.make_async_copy(hh, held.at[19:26], local.at[3])],
+             [pltpu.make_async_copy(cf, cfv, local.at[4]),
+              pltpu.make_async_copy(ch, chv, local.at[5])]]
+    for group in loads:
+        for copy in group:
+            copy.start()
     me = row_of(x, y, k)
     x_group = [row_of(x, (y + d) % 4, (k + dk) % 2) for d, dk in OFFSETS]
     y_group = [row_of((x + d) % 4, y, (k + dk) % 2) for d, dk in OFFSETS]
@@ -428,36 +429,37 @@
 
     entry = mask_ref[0] * RING + col
     word = table[0, entry]
-    odd = mask_ref[0] & 1
     ring = {}
 
-    def ring_send_slot(source, slot, s, device):
+    def ring_send_of(step, s):
         lo, hi = SPLITS[s]
-        ring[slot, s] = send(source.at[lo:hi], landing.at[slot, lo:hi],
-                             ring_send.at[slot, s], ring_recv.at[slot, s], device)
+        for way in range(2):
+            slot = way * STEPS + step
+            code = (word >> (3 * slot)) & 7
+            if step:
+                ring[slot - 1, s].wait_recv()
+            value = own[0, lo:hi]
+            for kind in RING_KINDS[slot]:
+                if kind == 1:
+                    value = jnp.where(code == 1, own[1, lo:hi], value)
+                elif kind:
+                    value = jnp.where(code == kind, landing[way * STEPS + kind - 2, lo:hi], value)
+            leaving[slot, lo:hi] = value
+            ring[slot, s] = send(leaving.at[slot, lo:hi], landing.at[slot, lo:hi],
+                                 ring_send.at[slot, s], ring_recv.at[slot, s],
+                                 (me, near_col[(1 - 2 * way) * JUMPS[step]]))
 
     def ring_step(step):
-        for s, (lo, hi) in enumerate(SPLITS):
-            if step == 0:
-                for h in range(2):
-                    ring[2 * STEPS + h, s].wait_recv()
-                    ready[h, lo:hi] = jnp.where(odd == 1, landing[2 * STEPS + h, lo:hi],
-                                                own[h, lo:hi])
-            for way in range(2):
-                slot = way * STEPS + step
-                code = (word >> (2 * slot)) & 3
-                other = ready[0, lo:hi]
-                if step:
-                    ring[slot - 1, s].wait_recv()
-                    other = jnp.where(code == 1, other, landing[slot - 1, lo:hi])
-                leaving[slot, lo:hi] = jnp.where(code == 2, ready[1, lo:hi], other)
-                ring_send_slot(leaving.at[slot], slot, s, (me, near_col[2 - 4 * way]))
-
-    pack_trade(hf, hh, own)
-    pl.semaphore_wait(barrier, len(greeted))
-    for s in range(len(SPLITS)):
-        for h in range(2):
-            ring_send_slot(own.at[h], 2 * STEPS + h, s, (me, near_col[1 - 2 * h]))
+        for s in range(len(SPLITS)):
+            ring_send_of(step, s)
+
+    for s, (lo, hi) in enumerate(SPLITS):
+        for copy in loads[s]:
+            copy.wait()
+        pack_trade(held, own, lo, hi)
+        if s == 0:
+            pl.semaphore_wait(barrier, len(greeted))
+        ring_send_of(0, s)
     code_copies = [send(codes_in, codes.at[n], code_send.at[n], code_recv.at[n], (peer, col))
                    for n, peer in enumerate(peers)]
 
@@ -467,14 +469,16 @@
         else:
             held_b[0, octant, 16 * (i - 4):16 * (i - 4) + 16, :] = value
 
-    pack_coarse(cf, ch, spread, put)
+    for copy in loads[3]:
+        copy.wait()
+    pack_coarse(cfv, chv, spread, put)
     one_copies = []
     for d in (2, 1, 3):
         one_copies.append(send(held_a.at[0], held_a.at[d], one_send.at[0, d], one_recv.at[0, d],
                                (row_of((x + d) % 4, y, k), col)))
         one_copies.append(send(held_b.at[0], held_b.at[d], one_send.at[1, d], one_recv.at[1, d],
                                (row_of(x, (y + d) % 4, k), col)))
-    ring_step(0)
+    ring_step(1)
 
     source = [codes_in[0, 0, j] for j in range(4)]
     refined = [jnp.where(v >= 0, 1, 0) for v in source]
@@ -484,14 +488,14 @@
     child = [jnp.where(refined[j] == 1, rank[j] * 8, 1 << 20) for j in range(4)]
     trade = jnp.where((moved[0, 0] > 0) & (refined[0] == 0), 0, 1 << 20)
     one_hots(children, trades, child, trade)
-    ring_step(1)
+    ring_step(2)
 
     for copy in code_copies + one_copies:
         copy.wait_recv()
     mine = first_and_last(source)
     two_copies = []
     for n, (d, dk) in enumerate(OFFSETS):
-        for part, (group, stage, got, held, home) in enumerate((
+        for part, (group, stage, got, parents, home) in enumerate((
                 (x_group, stage_a, got_a, held_a, x), (y_group, stage_b, got_b, held_b, y))):
             if n == 0:
                 pair = mine
@@ -501,7 +505,7 @@
                 pair = first_and_last([codes[row, 0, 0, j] for j in range(4)])
             for s, code in enumerate(pair):
                 parent = (code >> 6) & 3 if part == 0 else (code >> 4) & 3
-                value = held[(home - parent + 4) & 3, code & 7]
+                value = parents[(home - parent + 4) & 3, code & 7]
                 if n == 0:
                     got[0, s] = value
                 else:
@@ -509,8 +513,8 @@
             if n:
                 two_copies.append(send(stage.at[n], got.at[n], two_send.at[part, n],
                                        two_recv.at[part, n], (group[n], col)))
-    ring_step(2)
     ring_step(3)
+    ring_step(4)
 
     for copy in two_copies:
         copy.wait_recv()
@@ -532,7 +536,7 @@
             for rt in range(2):
                 rows = slice(16 * p + 8 * rt, 16 * p + 8 * rt + 8)
                 fresh[rows, cols] = jnp.where(
-                    kept, held_tile(hf, hh, p, slice(8 * rt, 8 * rt + 8), cols),
+                    kept, held[p, 8 * rt:8 * rt + 8, cols],
                     fresh[rows, cols])
         return carry
 
@@ -547,13 +551,21 @@
         cols = slice(256 * t, 256 * t + 256)
         fresh[:, cols] += jnp.dot(left[...], trades[:, cols], preferred_element_type=F32)
 
-    def exchange(turn, faces, arrivals):
+    def trade_faces(turn, moves, first):
+        return [send(a, b, halo_send.at[turn, first + n], halo_recv.at[turn, first + n],
+                     (near_row[sx], near_col[sy])) for n, (a, b, sx, sy) in enumerate(moves)]
+
+    def step(turn, compute, field, base, lead, faces, arrivals):
         (xs, ys, cs), (xr, yr, cr) = faces, arrivals
+        lax.fori_loop(0, 2, lambda n, c: compute(7 - 7 * n, c), 0)
+        y_faces(field, ys, cs, base, lead)
         moves = [(cs.at[n], cr.at[n], sx, sy) for n, (p, sx, sy) in enumerate(CORNERS)]
-        moves += [(xs.at[0], xr.at[0], 1, 0), (xs.at[1], xr.at[1], -1, 0),
-                  (ys.at[0], yr.at[0], 0, 1), (ys.at[1], yr.at[1], 0, -1)]
-        return [send(a, b, halo_send.at[turn, n], halo_recv.at[turn, n],
-                     (near_row[sx], near_col[sy])) for n, (a, b, sx, sy) in enumerate(moves)]
+        moves += [(ys.at[0], yr.at[0], 0, 1), (ys.at[1], yr.at[1], 0, -1)]
+        copies = trade_faces(turn, moves, 0)
+        lax.fori_loop(1, 7, compute, 0)
+        x_faces(field, xs, base, lead)
+        return copies + trade_faces(
+            turn, [(xs.at[0], xr.at[0], 1, 0), (xs.at[1], xr.at[1], -1, 0)], 6)
 
     def first_step(t, carry):
         cols = pl.ds(pl.multiple_of(128 * t, 128), 128)
@@ -564,12 +576,6 @@
                 wide[p, 8 + 8 * rt:16 + 8 * rt, wide_cols] = value
         return carry
 
-    lax.fori_loop(0, 8, first_step, 0)
-    edge_faces(wide, xs1, ys1, cs1, 8, 128)
-    for copy in exchange(0, (xs1, ys1, cs1), (xr1, yr1, cr1)):
-        copy.wait_recv()
-    fill_edges(xr1, yr1, cr1, wide)
-
     def second_step(t, carry):
         cols = pl.ds(pl.multiple_of(128 * t, 128), 128)
         for rt in range(2):
@@ -578,33 +584,50 @@
                 relaxed[p, 8 * rt:8 * rt + 8, cols] = value
         return carry
 
-    lax.fori_loop(0, 8, second_step, 0)
-    edge_faces(relaxed, xs2, ys2, cs2, 0, 0)
-    for copy in exchange(1, (xs2, ys2, cs2), (xr2, yr2, cr2)):
+    arrivals = (xr1, yr1, cr1)
+    for copy in step(0, first_step, wide, 8, 128, (xs1, ys1, cs1), arrivals):
+        copy.wait_recv()
+    fill_edges(xr1, yr1, cr1, wide)
+    copies = step(1, second_step, relaxed, 0, 0, (xs2, ys2, cs2), (xr2, yr2, cr2))
+    store = pltpu.make_async_copy(relaxed, relaxed_out, local.at[6])
+    store.start()
+    for copy in copies:
         copy.wait_recv()
     for copy in pending:
         copy.wait_send()
-
-
-def final_kernel(relaxed_in, xr, yr, cr, out_flow, out_heat, wide):
-    widen(relaxed_in, xr, yr, cr, wide)
-
-    def body(k, carry):
-        cols = pl.ds(pl.multiple_of(128 * k, 128), 128)
-        for rt in range(2):
-            for p in range(NPOP):
-                value = pulled(wide, p, rt, k)
-                if p < 19:
-                    out_flow[p, 8 * rt:8 * rt + 8, cols] = value
-                else:
-                    out_heat[p - 19, 8 * rt:8 * rt + 8, cols] = value
-        return carry
-
-    lax.fori_loop(0, 8, body, 0)
+    store.wait()
+
+
+FINAL_GROUPS = ((0, 7), (7, 11), (11, 15), (15, 19), (19, 26))
+
+
+def final_kernel(relaxed, xr, yr, cr, out_flow, out_heat, wide, result, load, store):
+    loads = []
+    for n, (lo, hi) in enumerate(FINAL_GROUPS):
+        copy = pltpu.make_async_copy(relaxed.at[lo:hi],
+                                     wide.at[lo:hi, 8:24, 128:128 + LANES], load.at[n])
+        copy.start()
+        loads.append(copy)
+    fill_edges(xr, yr, cr, wide)
+    stores = []
+    for n, (lo, hi) in enumerate(FINAL_GROUPS):
+        loads[n].wait()
+
+        for p in range(lo, hi):
+            for rt in range(2):
+                for t in range(8):
+                    result[p, 8 * rt:8 * rt + 8, 128 * t:128 * t + 128] = pulled(wide, p, rt, t)
+        target = out_flow.at[lo:hi] if hi <= 19 else out_heat
+        copy = pltpu.make_async_copy(result.at[lo:hi], target, store.at[n])
+        copy.start()
+        stores.append(copy)
+    for copy in stores:
+        copy.wait()
 
 
 VMEM = pl.BlockSpec(memory_space=pltpu.VMEM)
 SMEM = pl.BlockSpec(memory_space=pltpu.SMEM)
+ANY = pl.BlockSpec(memory_space=pl.ANY)
 
 
 def struct(shape, dtype=F32):
@@ -616,10 +639,9 @@
 WIDE = pltpu.VMEM((NPOP, 32, LANES + 256), F32)
 
 
-def call(kernel, ins, outs, scratch, **params):
+def call(kernel, ins, outs, places, scratch, **params):
     return pl.pallas_call(
-        kernel, out_shape=outs, in_specs=ins,
-        out_specs=jax.tree.map(lambda _: VMEM, outs), scratch_shapes=scratch,
+        kernel, out_shape=outs, in_specs=ins, out_specs=places, scratch_shapes=scratch,
         compiler_params=pltpu.CompilerParams(vmem_limit_bytes=56 * 2**20, **params))
 
 
@@ -630,12 +652,14 @@
 def per_device(held_flow, held_heat, coarse_flow, coarse_heat, pair_mask, moved_count, refine_src):
     dma = pltpu.SemaphoreType.DMA
     ns = len(SPLITS)
-    slots = 2 * STEPS + 2
+    slots = 2 * STEPS
+    field = pltpu.VMEM((NPOP, LX, LANES), F32)
     block = (NPOP, LX, 128)
     relaxed, *faces = call(
-        main_kernel, [SMEM] * 4 + [VMEM] * 4, [FIELD] + FACES,
-        [pltpu.VMEM((2,) + block, BF16), pltpu.VMEM((slots,) + block, BF16),
-         pltpu.VMEM((2 * STEPS,) + block, BF16), pltpu.VMEM((2,) + block, BF16),
+        main_kernel, [SMEM] * 4 + [ANY] * 4, [FIELD] + FACES, [ANY] + [VMEM] * 3,
+        [field, pltpu.VMEM((19, 4096), BF16), pltpu.VMEM((7, 4096), BF16), field,
+         pltpu.VMEM((2,) + block, BF16), pltpu.VMEM((slots,) + block, BF16),
+         pltpu.VMEM((slots,) + block, BF16),
          pltpu.VMEM((4, 8, ROWS_A, 128), BF16), pltpu.VMEM((4, 8, ROWS_B, 128), BF16),
          pltpu.SMEM((13, 1, 1, 4), jnp.int32),
          pltpu.VMEM((8, 2, ROWS_A, 128), BF16), pltpu.VMEM((8, 2, ROWS_B, 128), BF16),
@@ -646,12 +670,14 @@
          pltpu.VMEM((NPOP * LX, LANES), F32), WIDE]
         + [vmem(f) for f in FACES * 3]
         + [dma((slots, ns)), dma((slots, ns)), dma((13,)), dma((13,)),
-           dma((2, 4)), dma((2, 4)), dma((2, 8)), dma((2, 8)), dma((2, 8)), dma((2, 8))],
+           dma((2, 4)), dma((2, 4)), dma((2, 8)), dma((2, 8)), dma((2, 8)), dma((2, 8)), dma((7,))],
         collective_id=0, has_side_effects=True)(
             jnp.asarray(RING_TABLE), pair_mask, moved_count, refine_src,
             held_flow, held_heat, coarse_flow.reshape(19, 4096), coarse_heat.reshape(7, 4096))
-    return tuple(call(final_kernel, [VMEM] * 4,
-                      [struct((19, LX, LANES)), struct((7, LX, LANES))], [WIDE])(relaxed, *faces))
+    groups = len(FINAL_GROUPS)
+    return tuple(call(
+        final_kernel, [ANY] + [VMEM] * 3, [struct((19, LX, LANES)), struct((7, LX, LANES))],
+        [ANY] * 2, [WIDE, field, dma((groups,)), dma((groups,))])(relaxed, *faces))
 
 
 def solution(mesh):

time: 62 us -> 57.6 us (0.929)
  Pallas kernels: 59.9 us -> 55.4 us
    pallas_call x2, Pallas kernels: 59.9 us -> 55.4 us  [the longest x1 52 us: per_device(): call(main_kernel, [SMEM] * 4 + [ANY] * 4, [FIELD] + FACES, [ANY] + [VMEM]...]
where the time goes in v3:
time: 57.6 us; the launch traced here: 57.3 us
  Pallas kernels  55.4 us (96%)
  between operations  1.93 us (3%)
    pallas_call x1, Pallas kernels, per_device(): call(main_kernel, [SMEM] * 4 + [ANY] * 4, [FIELD] + FACES, [ANY] + [VMEM]...  52 us
    pallas_call x1, Pallas kernels, per_device(): call(final_kernel, [ANY] + [VMEM] * 3, [struct((19, LX, LANES)), struct((...  3.43 us

profile of v3, /device:TPU:32, one launch (start us, length us, event | category | flops | bytes accessed | tf_op | source)
XLA Modules:
  0.0 57.3 jit_solution(15331142323774368906)
XLA Ops:
  1.9 52.0 %shard_map.95 = (f32[26,16,1024]{2,1,0:T(8,128)}, f32[2,8,1024]{2,1,0:T(8,128)}, f32[2,3,16,128]{3,2,1,0:T(8,128)}, f32[4,8,128]{2,1,0:T(8,128)}) custom-call(s32[3,256]{1,0:T(4,128)} %constant.2.clone.table, s32[1]{0:T(128)S(6)} %copy.10.mask_ref, s32[1,1]{1,0:T(1,128)S(6)} %copy.11.moved, s32[1,1,4]{2,1,0:T(1,128)} %codes_in.1, f32[19,16,1024]{2,1,0:T(8,128)} %hf.1, ...), custom_call_target="tpu_custom_call" | custom-call | tf_op jit(solution)/shard_map/pallas_call | solution.py:658
  53.9 3.4 %shard_map.96 = (f32[19,16,1024]{2,1,0:T(8,128)}, f32[7,16,1024]{2,1,0:T(8,128)}) custom-call(f32[26,16,1024]{2,1,0:T(8,128)} %get-tuple-element.6.relaxed, f32[2,8,1024]{2,1,0:T(8,128)} %get-tuple-element.7.xr, f32[2,3,16,128]{3,2,1,0:T(8,128)} %get-tuple-element.8.yr, f32[4,8,128]{2,1,0:T(8,128)} %get-tuple-element.9.cr), custom_call_target="tpu_custom_call" | custom-call | tf_op jit(solution)/shard_map/pallas_call | solution.py:678

commit v4 on v3

--- a/solution.py
+++ b/solution.py
@@ -386,24 +386,15 @@
         left[rows, 128:256] = (value - top.astype(F32)).astype(BF16)
 
 
-def main_kernel(table, mask_ref, moved, codes_in, hf, hh, cf, ch,
+def main_kernel(table_in, mask_in, moved_in, codes_all, hf, hh, cf, ch,
                 relaxed_out, xr2, yr2, cr2,
-                held, cfv, chv, relaxed, own, landing, leaving, held_a, held_b, codes,
+                table, mask_ref, moved, codes_in, held, cfv, chv, relaxed, own, landing, leaving, held_a, held_b, codes,
                 stage_a, stage_b, got_a, got_b, picked_a, picked_b,
                 spread, left, children, trades, fresh, wide,
                 xs1, ys1, cs1, xr1, yr1, cr1, xs2, ys2, cs2,
                 ring_send, ring_recv, code_send, code_recv, one_send, one_recv,
                 two_send, two_recv, halo_send, halo_recv, local):
     x, y, k, col = place()
-    loads = [[pltpu.make_async_copy(hf.at[0:9], held.at[0:9], local.at[0])],
-             [pltpu.make_async_copy(hf.at[9:18], held.at[9:18], local.at[1])],
-             [pltpu.make_async_copy(hf.at[18:19], held.at[18:19], local.at[2]),
-              pltpu.make_async_copy(hh, held.at[19:26], local.at[3])],
-             [pltpu.make_async_copy(cf, cfv, local.at[4]),
-              pltpu.make_async_copy(ch, chv, local.at[5])]]
-    for group in loads:
-        for copy in group:
-            copy.start()
     me = row_of(x, y, k)
     x_group = [row_of(x, (y + d) % 4, (k + dk) % 2) for d, dk in OFFSETS]
     y_group = [row_of((x + d) % 4, y, (k + dk) % 2) for d, dk in OFFSETS]
@@ -414,8 +405,20 @@
     barrier = pltpu.get_barrier_semaphore()
     greeted = [(me, near_col[d]) for d in (-2, -1, 1, 2)] + [(peer, col) for peer in peers]
     greeted += [(near_row[sx], near_col[sy]) for sx in (-1, 1) for sy in (-1, 0, 1)]
-    for device in greeted:
+    for device in reversed(greeted):
         pl.semaphore_signal(barrier, inc=1, device_id=device, device_id_type=MESH)
+
+    def load(source, target, n):
+        copy = pltpu.make_async_copy(source, target, local.at[n])
+        copy.start()
+        return copy
+
+    scalars = [load(table_in, table, 7), load(mask_in, mask_ref, 8),
+               load(moved_in, moved, 9), load(codes_all, codes_in, 10)]
+    loads = [[load(hf.at[0:9], held.at[0:9], 0)],
+             [load(hf.at[9:18], held.at[9:18], 1)],
+             [load(hf.at[18:19], held.at[18:19], 2), load(hh, held.at[19:26], 3)],
+             [load(cf, cfv, 4), load(ch, chv, 5)]]
 
     pending = []
 
@@ -427,6 +430,8 @@
         pending.append(copy)
         return copy
 
+    for copy in scalars:
+        copy.wait()
     entry = mask_ref[0] * RING + col
     word = table[0, entry]
     ring = {}
@@ -547,37 +552,37 @@
             ring[way * STEPS + STEPS - 1, s].wait_recv()
     for h in range(2):
         left[:, 128 * h:128 * h + 128] = landing[table[1 + h, entry]].reshape(NPOP * LX, 128)
-    for t in range(4):
-        cols = slice(256 * t, 256 * t + 256)
-        fresh[:, cols] += jnp.dot(left[...], trades[:, cols], preferred_element_type=F32)
-
     def trade_faces(turn, moves, first):
         return [send(a, b, halo_send.at[turn, first + n], halo_recv.at[turn, first + n],
                      (near_row[sx], near_col[sy])) for n, (a, b, sx, sy) in enumerate(moves)]
 
     def step(turn, compute, field, base, lead, faces, arrivals):
         (xs, ys, cs), (xr, yr, cr) = faces, arrivals
-        lax.fori_loop(0, 2, lambda n, c: compute(7 - 7 * n, c), 0)
+        compute(7, 0)
+        compute(0, 0)
         y_faces(field, ys, cs, base, lead)
         moves = [(cs.at[n], cr.at[n], sx, sy) for n, (p, sx, sy) in enumerate(CORNERS)]
         moves += [(ys.at[0], yr.at[0], 0, 1), (ys.at[1], yr.at[1], 0, -1)]
         copies = trade_faces(turn, moves, 0)
-        lax.fori_loop(1, 7, compute, 0)
+        for t in range(1, 7):
+            compute(t, 0)
         x_faces(field, xs, base, lead)
         return copies + trade_faces(
             turn, [(xs.at[0], xr.at[0], 1, 0), (xs.at[1], xr.at[1], -1, 0)], 6)
 
     def first_step(t, carry):
-        cols = pl.ds(pl.multiple_of(128 * t, 128), 128)
-        wide_cols = pl.ds(pl.multiple_of(128 * t + 128, 128), 128)
+        cols = slice(128 * t, 128 * t + 128)
+        wide_cols = slice(128 * t + 128, 128 * t + 256)
+        came = jnp.dot(left[...], trades[:, cols], preferred_element_type=F32)
         for rt in range(2):
-            f = [fresh[16 * p + 8 * rt:16 * p + 8 * rt + 8, cols] for p in range(NPOP)]
+            f = [fresh[16 * p + 8 * rt:16 * p + 8 * rt + 8, cols]
+                 + came[16 * p + 8 * rt:16 * p + 8 * rt + 8] for p in range(NPOP)]
             for p, value in enumerate(collide(f)):
                 wide[p, 8 + 8 * rt:16 + 8 * rt, wide_cols] = value
         return carry
 
     def second_step(t, carry):
-        cols = pl.ds(pl.multiple_of(128 * t, 128), 128)
+        cols = slice(128 * t, 128 * t + 128)
         for rt in range(2):
             f = [pulled(wide, p, rt, t) for p in range(NPOP)]
             for p, value in enumerate(collide(f)):
@@ -601,13 +606,21 @@
 FINAL_GROUPS = ((0, 7), (7, 11), (11, 15), (15, 19), (19, 26))
 
 
-def final_kernel(relaxed, xr, yr, cr, out_flow, out_heat, wide, result, load, store):
+def final_kernel(relaxed, xr_in, yr_in, cr_in, out_flow, out_heat,
+                 wide, result, xr, yr, cr, load, store):
+    faces = []
+    for n, (source, target) in enumerate(((xr_in, xr), (yr_in, yr), (cr_in, cr))):
+        copy = pltpu.make_async_copy(source, target, load.at[len(FINAL_GROUPS) + n])
+        copy.start()
+        faces.append(copy)
     loads = []
     for n, (lo, hi) in enumerate(FINAL_GROUPS):
         copy = pltpu.make_async_copy(relaxed.at[lo:hi],
                                      wide.at[lo:hi, 8:24, 128:128 + LANES], load.at[n])
         copy.start()
         loads.append(copy)
+    for copy in faces:
+        copy.wait()
     fill_edges(xr, yr, cr, wide)
     stores = []
     for n, (lo, hi) in enumerate(FINAL_GROUPS):
@@ -625,9 +638,8 @@
         copy.wait()
 
 
-VMEM = pl.BlockSpec(memory_space=pltpu.VMEM)
-SMEM = pl.BlockSpec(memory_space=pltpu.SMEM)
 ANY = pl.BlockSpec(memory_space=pl.ANY)
+HBM = pl.BlockSpec(memory_space=pltpu.HBM)
 
 
 def struct(shape, dtype=F32):
@@ -656,8 +668,9 @@
     field = pltpu.VMEM((NPOP, LX, LANES), F32)
     block = (NPOP, LX, 128)
     relaxed, *faces = call(
-        main_kernel, [SMEM] * 4 + [ANY] * 4, [FIELD] + FACES, [ANY] + [VMEM] * 3,
-        [field, pltpu.VMEM((19, 4096), BF16), pltpu.VMEM((7, 4096), BF16), field,
+        main_kernel, [HBM] * 4 + [ANY] * 4, [FIELD] + FACES, [ANY] * 4,
+        [pltpu.SMEM((3, RING * RING), jnp.int32), pltpu.SMEM((1,), jnp.int32),
+         pltpu.SMEM((1, 1), jnp.int32), pltpu.SMEM((1, 1, 4), jnp.int32), field, pltpu.VMEM((19, 4096), BF16), pltpu.VMEM((7, 4096), BF16), field,
          pltpu.VMEM((2,) + block, BF16), pltpu.VMEM((slots,) + block, BF16),
          pltpu.VMEM((slots,) + block, BF16),
          pltpu.VMEM((4, 8, ROWS_A, 128), BF16), pltpu.VMEM((4, 8, ROWS_B, 128), BF16),
@@ -670,14 +683,14 @@
          pltpu.VMEM((NPOP * LX, LANES), F32), WIDE]
         + [vmem(f) for f in FACES * 3]
         + [dma((slots, ns)), dma((slots, ns)), dma((13,)), dma((13,)),
-           dma((2, 4)), dma((2, 4)), dma((2, 8)), dma((2, 8)), dma((2, 8)), dma((2, 8)), dma((7,))],
+           dma((2, 4)), dma((2, 4)), dma((2, 8)), dma((2, 8)), dma((2, 8)), dma((2, 8)), dma((11,))],
         collective_id=0, has_side_effects=True)(
             jnp.asarray(RING_TABLE), pair_mask, moved_count, refine_src,
             held_flow, held_heat, coarse_flow.reshape(19, 4096), coarse_heat.reshape(7, 4096))
     groups = len(FINAL_GROUPS)
     return tuple(call(
-        final_kernel, [ANY] + [VMEM] * 3, [struct((19, LX, LANES)), struct((7, LX, LANES))],
-        [ANY] * 2, [WIDE, field, dma((groups,)), dma((groups,))])(relaxed, *faces))
+        final_kernel, [ANY] * 4, [struct((19, LX, LANES)), struct((7, LX, LANES))],
+        [ANY] * 2, [WIDE, field] + [vmem(f) for f in FACES] + [dma((groups + 3,)), dma((groups,))])(relaxed, *faces))
 
 
 def solution(mesh):

time: 57.6 us -> 55 us (0.955)
  Pallas kernels: 55.4 us -> 52.9 us
    pallas_call x2, Pallas kernels: 55.4 us -> 52.9 us  [the longest x1 50.2 us: per_device(): call(main_kernel, [HBM] * 4 + [ANY] * 4, [FIELD] + FACES, [ANY] * 4, [plt...]
where the time goes in v4:
time: 55 us; the launch traced here: 54.8 us
  Pallas kernels  52.9 us (96%)
  between operations  1.93 us (4%)
    pallas_call x1, Pallas kernels, per_device(): call(main_kernel, [HBM] * 4 + [ANY] * 4, [FIELD] + FACES, [ANY] * 4, [plt...  50.2 us
    pallas_call x1, Pallas kernels, per_device(): call(final_kernel, [ANY] * 4, [struct((19, LX, LANES)), struct((7, LX, LA...  2.67 us

profile of v4, /device:TPU:32, one launch (start us, length us, event | category | flops | bytes accessed | tf_op | source)
XLA Modules:
  0.0 54.8 jit_solution(264554441685206996)
XLA Ops:
  1.9 50.2 %shard_map.95 = (f32[26,16,1024]{2,1,0:T(8,128)}, f32[2,8,1024]{2,1,0:T(8,128)}, f32[2,3,16,128]{3,2,1,0:T(8,128)}, f32[4,8,128]{2,1,0:T(8,128)}) custom-call(s32[3,256]{1,0:T(4,128)} %constant.2.clone.table_in, s32[1]{0:T(128)S(6)} %copy.10.mask_in, s32[1,1]{1,0:T(1,128)S(6)} %copy.11.moved_in, s32[1,1,4]{2,1,0:T(1,128)} %codes_all.1, f32[19,16,1024]{2,1,0:T(8,128)} %hf.1, ...), custom_call_target="tpu_custom_call" | custom-call | tf_op jit(solution)/shard_map/pallas_call | solution.py:670
  52.1 2.7 %shard_map.96 = (f32[19,16,1024]{2,1,0:T(8,128)}, f32[7,16,1024]{2,1,0:T(8,128)}) custom-call(f32[26,16,1024]{2,1,0:T(8,128)} %get-tuple-element.6.relaxed, f32[2,8,1024]{2,1,0:T(8,128)} %get-tuple-element.7.xr_in, f32[2,3,16,128]{3,2,1,0:T(8,128)} %get-tuple-element.8.yr_in, f32[4,8,128]{2,1,0:T(8,128)} %get-tuple-element.9.cr_in), custom_call_target="tpu_custom_call" | custom-call | tf_op jit(solution)/shard_map/pallas_call | solution.py:691
